TPU v7x, 32 devices: a whole 2x2x4 slice. The times are simulated.
32 devices in a mesh: dp: 8 (over y, x, core), seq: 4 (over z).
Axes of the slice: x: 2, y: 2, z: 4, core: 2. Of those that a mesh axis runs over, the one named last changes fastest.
Arguments:
- values: bfloat16 [8, 1024, 512], P('dp', 'seq'), may hold values from -6 to 6
- gates_first: bfloat16 [8, 1024, 512], P('dp', 'seq'), may hold values from -6 to 6
- gates_second: bfloat16 [8, 1024, 512], P('dp', 'seq'), may hold values from -6 to 6
- filter_early: float32 [1024, 512], P('seq'), may hold values from -4 to 4
- filter_late: float32 [1024, 512], P('seq'), may hold values from -4 to 4
- skip_early: float32 [1024], P('seq'), may hold values from 0.1 to 1.9
- skip_late: float32 [1024], P('seq'), may hold values from 0.1 to 1.9
- targets: bfloat16 [8, 512, 1024], P('dp', 'seq'), may hold values from -6 to 6
- negative_rows: int32 [8, 8, 100], P('dp', 'seq'), may hold values from 0 to 1023
- recording_ids: int32 [8], replicated, may hold values from 0 to 3
Outputs:
- values_grad: bfloat16 [8, 1024, 512], P('dp', 'seq')
- first_grad: bfloat16 [8, 1024, 512], P('dp', 'seq')
- second_grad: bfloat16 [8, 1024, 512], P('dp', 'seq')
- early_grad: float32 [1024, 512], P('seq')
- late_grad: float32 [1024, 512], P('seq')
All inputs are finite; a program needn't handle non-finite values.
Results may differ from a plain program's by a relative error of at most 0.014.
Values may be sent and summed in bfloat16 or wider, within the bound.
A program may use at most 128 MiB of HBM per device.

v0:
```python
import functools
import math

import jax
import jax.numpy as jnp
import numpy as np
from jax import lax
from jax.experimental import pallas as pl
from jax.experimental.pallas import tpu as pltpu
from jax.sharding import PartitionSpec as P

EPSILON = 1e-06
INVERSE_TEMP = 10.0
LOSS_SCALE = 256.0
MESH = pl.DeviceIdType.MESH
F32 = jnp.float32
BF16 = jnp.bfloat16
TABLE_BYTES = 16 * 1024 * 1024
INNER_WIDTH = 128
HIGHEST = lax.Precision.HIGHEST


def shortened(value):

    def short(part):
        return part.astype(jnp.bfloat16) if part.dtype == jnp.float32 else part

    return jax.tree.map(short, value)


def twiddle(row_count, column_count, length, direction):
    product = (
        jnp.arange(row_count, dtype=jnp.int32)[:, None]
        * jnp.arange(column_count, dtype=jnp.int32)[None, :]
        % length
    )
    angles = direction * 2.0 * math.pi / length * product.astype(jnp.float32)
    return (jnp.cos(angles), jnp.sin(angles))


def complex_table(cosines, sines, with_imaginary):
    upper = jnp.concatenate([cosines, sines], axis=1)
    if not with_imaginary:
        return upper
    lower = jnp.concatenate([-sines, cosines], axis=1)
    return jnp.concatenate([upper, lower], axis=0)


def transform(real_part, imaginary, direction, length):
    used = real_part.shape[-1]
    with_imaginary = imaginary is not None
    outer_size = length // INNER_WIDTH
    used_rows = used // INNER_WIDTH
    lead = real_part.shape[:-1]
    folded_real = real_part.reshape(lead + (used_rows, INNER_WIDTH))
    cosines, sines = twiddle(used_rows, outer_size, outer_size, direction)
    table = complex_table(cosines, sines, with_imaginary)
    if with_imaginary:
        stacked = jnp.concatenate(
            [folded_real, imaginary.reshape(lead + (used_rows, INNER_WIDTH))], axis=-2
        )
    else:
        stacked = folded_real
    section = jnp.einsum("...ab,ak->...kb", stacked, table, precision=HIGHEST)
    section_real = section[..., :outer_size, :]
    section_imaginary = section[..., outer_size:, :]
    turn_cosine, turn_sine = twiddle(outer_size, INNER_WIDTH, length, direction)
    turned_real = section_real * turn_cosine - section_imaginary * turn_sine
    turned_imaginary = section_real * turn_sine + section_imaginary * turn_cosine
    inner_cosine, inner_sine = twiddle(INNER_WIDTH, INNER_WIDTH, INNER_WIDTH, direction)
    inner_table = complex_table(inner_cosine, inner_sine, True)
    second = jnp.einsum(
        "...ab,bk->...ak",
        jnp.concatenate([turned_real, turned_imaginary], axis=-1),
        inner_table,
        precision=HIGHEST,
    )
    final_real = jnp.swapaxes(second[..., :INNER_WIDTH], -1, -2).reshape(lead + (length,))
    final_imaginary = jnp.swapaxes(second[..., INNER_WIDTH:], -1, -2).reshape(lead + (length,))
    return (final_real, final_imaginary)


def spectrum(signal):
    return transform(signal, None, -1.0, 2 * signal.shape[-1])


def split_pair(first_signal, second_signal):
    spec_real, spec_imaginary = transform(
        first_signal, second_signal, -1.0, 2 * first_signal.shape[-1]
    )
    mirror_real = jnp.roll(jnp.flip(spec_real, -1), 1, -1)
    mirror_imaginary = jnp.roll(jnp.flip(spec_imaginary, -1), 1, -1)
    first_spec = ((spec_real + mirror_real) * 0.5, (spec_imaginary - mirror_imaginary) * 0.5)
    second_spec = ((spec_imaginary + mirror_imaginary) * 0.5, (mirror_real - spec_real) * 0.5)
    return (first_spec, second_spec)


def multiply(left_side, right_side):
    return (
        left_side[0] * right_side[0] - left_side[1] * right_side[1],
        left_side[0] * right_side[1] + left_side[1] * right_side[0],
    )


def conjugate(spec):
    return (spec[0], -spec[1])


def combine(left_side, right_side):
    return (left_side[0] - right_side[1], left_side[1] + right_side[0])


def inverse(spec, frames):
    length = spec[0].shape[-1]
    out_real, out_imaginary = transform(spec[0], spec[1], 1.0, length)
    factor = 1.0 / length
    return (out_real[..., :frames] * factor, out_imaginary[..., :frames] * factor)


def local_large(
    values,
    gates_first,
    gates_second,
    filter_early,
    filter_late,
    skip_early,
    skip_late,
    targets,
    negative_rows,
    recording_ids,
):
    signal = values[0].astype(jnp.float32)
    inner_gate = gates_first[0].astype(jnp.float32)
    outer_gate = gates_second[0].astype(jnp.float32)
    frames = signal.shape[-1]
    early_skip = skip_early[:, None]
    late_skip = skip_late[:, None]
    target_full = targets[0].astype(jnp.float32)
    unit_target = (
        target_full / jnp.sqrt(jnp.sum(target_full * target_full, axis=-1, keepdims=True) + EPSILON)
    ).astype(jnp.bfloat16)
    signal_spec, early_spec = split_pair(signal, filter_early)
    mixed_one = inverse(multiply(signal_spec, early_spec), frames)[0] + early_skip * signal
    hidden = inner_gate * mixed_one
    hidden_spec, late_spec = split_pair(hidden, filter_late)
    mixed_two = inverse(multiply(hidden_spec, late_spec), frames)[0] + late_skip * hidden
    output = outer_gate * mixed_two
    arrived = lax.all_to_all(
        output[None].astype(jnp.bfloat16), "seq", split_axis=2, concat_axis=1, tiled=True
    ).astype(jnp.float32)
    output_rows = jnp.transpose(arrived[0])
    radius = jnp.sqrt(jnp.sum(output_rows * output_rows, axis=-1, keepdims=True) + EPSILON)
    unit_rows = output_rows / radius
    anchors = unit_rows.astype(jnp.bfloat16)
    own_record = lax.axis_index("dp")
    record_count = recording_ids.shape[0]
    record_range = jnp.arange(record_count, dtype=jnp.int32)
    self_label = jnp.sum(jnp.where(record_range == own_record, recording_ids, 0))
    segment = anchors.shape[0]
    block_rows = negative_rows[0]
    block_count = block_rows.shape[0]
    block_size = segment // block_count
    column_ids = jnp.arange(segment, dtype=jnp.int32)
    initial = (
        jnp.zeros((segment,), jnp.float32),
        jnp.zeros((segment, anchors.shape[1]), jnp.float32),
    )
    shard_rows = lax.all_gather(unit_target[None], "dp", axis=0, tiled=True)

    def one_record(partial_value, member):
        pool_rows, record = member
        label = jnp.sum(jnp.where(record_range == record, recording_ids, 0))
        allowed = (label != self_label).astype(jnp.float32)
        matches = (block_rows[:, :, None] == (record * segment + column_ids)[None, None, :]).astype(
            jnp.float32
        )
        counts = jnp.sum(matches, axis=1) * allowed
        counts = jnp.broadcast_to(counts[:, None, :], (block_count, block_size, segment)).reshape(
            segment, segment
        )
        scores = (
            lax.dot_general(
                anchors, pool_rows, (((1,), (1,)), ((), ())), preferred_element_type=jnp.float32
            )
            * INVERSE_TEMP
        )
        weights = counts * jnp.exp(scores)
        numerator = jnp.dot(
            weights.astype(jnp.bfloat16), pool_rows, preferred_element_type=jnp.float32
        )
        return ((partial_value[0] + jnp.sum(weights, axis=-1), partial_value[1] + numerator), None)

    records = jnp.arange(shard_rows.shape[0], dtype=jnp.int32)
    summed = lax.scan(one_record, initial, (shard_rows, records))[0]
    unit_self = unit_target.astype(jnp.float32)
    positive = jnp.exp(jnp.sum(anchors.astype(jnp.float32) * unit_self, axis=-1) * INVERSE_TEMP)
    totals = positive + summed[0]
    anchor_grad = ((positive / totals - 1.0)[:, None] * unit_self + summed[1] / totals[:, None]) * (
        INVERSE_TEMP * LOSS_SCALE
    )
    frame_grad = (
        anchor_grad - unit_rows * jnp.sum(unit_rows * anchor_grad, axis=-1, keepdims=True)
    ) / radius
    arrived_back = lax.all_to_all(
        shortened(jnp.transpose(frame_grad)[None]), "seq", split_axis=1, concat_axis=2, tiled=True
    )
    cotangent = arrived_back[0]
    second_grad = (cotangent * mixed_two).astype(jnp.bfloat16)
    late_drive = cotangent * outer_gate
    back_late = spectrum(late_drive)
    late_pair = combine(
        multiply(back_late, conjugate(late_spec)), multiply(back_late, conjugate(hidden_spec))
    )
    hidden_back, late_update = inverse(late_pair, frames)
    hidden_grad = hidden_back + late_skip * late_drive
    first_grad = (hidden_grad * mixed_one).astype(jnp.bfloat16)
    early_drive = hidden_grad * inner_gate
    back_early = spectrum(early_drive)
    early_pair = combine(
        multiply(back_early, conjugate(early_spec)), multiply(back_early, conjugate(signal_spec))
    )
    signal_back, early_update = inverse(early_pair, frames)
    values_grad = (signal_back + early_skip * early_drive).astype(jnp.bfloat16)
    filter_sums = (
        lax.psum(early_update.astype(jnp.bfloat16), "dp").astype(jnp.float32),
        lax.psum(late_update.astype(jnp.bfloat16), "dp").astype(jnp.float32),
    )
    return (
        values_grad[None],
        first_grad[None],
        second_grad[None],
        filter_sums[0] / frames,
        filter_sums[1] / frames,
    )


def tables(frames):
    odd = 2 * np.arange(frames, dtype=np.int64) + 1
    period = 8 * frames
    circle = 2.0 * np.pi / period * np.arange(period)
    product = odd[:, None] * odd[None, :] % period
    highs, lows = [], []
    for wave in (np.cos(circle), np.sin(circle)):
        wave = wave.astype(np.float32)
        high = wave.astype(BF16)
        low = (wave - high.astype(np.float32)).astype(BF16)
        highs.append(high[product])
        lows.append(low[product])
    half = np.pi * odd / (4.0 * frames)
    turn = np.stack([np.cos(half), np.sin(half)]) / frames
    return np.stack(highs), np.stack(lows), turn.astype(np.float32)


def halves(value):
    high = value.astype(BF16)
    return high, (value - high.astype(F32)).astype(BF16)


def product(parts, table_high, table_low):
    high, low = parts
    total = jnp.dot(high, table_high, preferred_element_type=F32)
    if table_low is not None:
        total += jnp.dot(high, table_low, preferred_element_type=F32)
    if low is not None:
        total += jnp.dot(low, table_high, preferred_element_type=F32)
    return total


def kernel(
    sizes,
    values_ref, first_ref, second_ref, early_ref, late_ref, early_skip_ref, late_skip_ref,
    targets_ref, rows_ref, ids_ref, high_ref, low_ref, turn_ref,
    values_out, first_out, second_out, early_out, late_out,
    pool, out_send, out_recv, back_send, back_recv, reduce_send, reduce_recv,
    mixed_one, mixed_two, early_spec, late_spec, signal_spec, hidden_spec,
    pool_send_sem, pool_recv_sem, pass_send_sem, pass_recv_sem,
    out_send_sem, out_recv_sem, back_send_sem, back_recv_sem,
    reduce_send_sem, reduce_recv_sem, share_send_sem, share_recv_sem,
):
    records, stages = sizes
    chips = records // 2
    me = lax.axis_index("dp")
    here = lax.axis_index("seq")
    chip, core = me // 2, me % 2
    partner = chip * 2 + (1 - core)
    channels, frames = mixed_one.shape
    segment = pool.shape[1]
    depth = pool.shape[2]

    barrier = pltpu.get_barrier_semaphore()
    for k in range(1, records):
        pl.semaphore_signal(
            barrier, inc=1, device_id=(lax.rem(me + k, records), here), device_id_type=MESH
        )
    for k in range(1, stages):
        pl.semaphore_signal(
            barrier, inc=1, device_id=(me, lax.rem(here + k, stages)), device_id_type=MESH
        )

    def remote(source, target, send, recv, device):
        return pltpu.make_async_remote_copy(
            src_ref=source, dst_ref=target, send_sem=send, recv_sem=recv,
            device_id=device, device_id_type=MESH,
        )

    full = targets_ref[0].astype(F32)
    norm = jnp.sqrt(jnp.sum(full * full, axis=-1, keepdims=True) + EPSILON)
    pool[me] = (full / norm).astype(BF16)
    pl.semaphore_wait(barrier, records + stages - 2)

    def pool_copy(k):
        peer = lax.rem(chip + k, chips) * 2 + core
        return remote(pool.at[me], pool.at[me], pool_send_sem.at[k], pool_recv_sem.at[k], (peer, here))

    def pool_arrival(k):
        slot = lax.rem(chip + chips - k, chips) * 2 + core
        return slot, remote(
            pool.at[slot], pool.at[slot], pool_send_sem.at[k], pool_recv_sem.at[k], (slot, here)
        )

    def pass_copy(k):
        slot = lax.rem(chip + chips - k, chips) * 2 + core
        return remote(
            pool.at[slot], pool.at[slot], pass_send_sem.at[k], pass_recv_sem.at[k], (partner, here)
        )

    def pass_arrival(k):
        slot = lax.rem(chip + chips - k, chips) * 2 + (1 - core)
        return remote(
            pool.at[slot], pool.at[slot], pass_send_sem.at[k], pass_recv_sem.at[k], (partner, here)
        )

    for k in range(1, chips):
        pool_copy(k).start()
    pass_copy(0).start()

    def forward(parts):
        return tuple(product(parts, high_ref[i], low_ref[i]) for i in (0, 1))

    def inverse(cosine, sine, fine=True):
        total = None
        for i, wave in enumerate((cosine, sine)):
            part = product((wave.astype(BF16), None), high_ref[i], low_ref[i] if fine else None)
            total = part if total is None else total + part
        return total

    def unshifted(spec):
        cosine, sine = spec
        turn_cosine = turn_ref[0:1, :]
        turn_sine = turn_ref[1:2, :]
        return (
            cosine * turn_cosine + sine * turn_sine,
            sine * turn_cosine - cosine * turn_sine,
        )

    def keep(ref, spec):
        ref[0] = spec[0]
        ref[1] = spec[1]

    def convolved(spec, ref):
        cosine, sine = spec
        return inverse(cosine * ref[0] - sine * ref[1], cosine * ref[1] + sine * ref[0])

    def correlated(spec, ref, fine=True):
        cosine, sine = spec
        return inverse(cosine * ref[0] + sine * ref[1], sine * ref[0] - cosine * ref[1], fine)

    def column(row):
        return jnp.broadcast_to(row, (8, channels)).T[:, 0:1]

    early_skip = column(early_skip_ref[...])
    late_skip = column(late_skip_ref[...])

    keep(early_spec, unshifted(forward(halves(early_ref[...]))))
    keep(late_spec, unshifted(forward(halves(late_ref[...]))))
    spec = forward((values_ref[0], None))
    mixed_one[...] = convolved(spec, early_spec) + early_skip * values_ref[0].astype(F32)
    signal_waves = spec
    hidden = first_ref[0].astype(F32) * mixed_one[...]
    spec = forward((hidden.astype(BF16), None))
    mixed_two[...] = convolved(spec, late_spec) + late_skip * hidden

    output = second_ref[0].astype(F32) * mixed_two[...]
    for s in range(stages):
        out_send[s] = output[:, s * segment : (s + 1) * segment].astype(BF16)

    def exchange(k, send, recv, send_sem, recv_sem):
        peer = lax.rem(here + k, stages)
        return remote(send.at[peer], recv.at[here], send_sem.at[k], recv_sem.at[k], (me, peer))

    def exchange_arrival(k, send, recv, send_sem, recv_sem):
        peer = lax.rem(here + stages - k, stages)
        return remote(send.at[peer], recv.at[peer], send_sem.at[k], recv_sem.at[k], (me, peer))

    out_group = (out_send, out_recv, out_send_sem, out_recv_sem)
    back_group = (back_send, back_recv, back_send_sem, back_recv_sem)
    for k in range(1, stages):
        exchange(k, *out_group).start()
    out_recv[here] = out_send[here]
    keep(signal_spec, unshifted(signal_waves))
    keep(hidden_spec, unshifted(spec))

    for k in range(1, chips):
        pool_arrival(k)[1].wait_recv()
        pass_copy(k).start()

    blocks = rows_ref.shape[1]
    draws = rows_ref.shape[2]
    block_size = segment // blocks
    frame_block = lax.broadcasted_iota(jnp.int32, (draws, segment), 1) // block_size
    counts = jnp.zeros((records * segment, segment), F32)
    position = lax.broadcasted_iota(jnp.int32, (records * segment, draws), 0)
    for b in range(blocks):
        matches = jnp.where(position == rows_ref[0, b : b + 1, :], 1.0, 0.0).astype(BF16)
        chosen = jnp.where(frame_block == b, 1.0, 0.0).astype(BF16)
        counts += jnp.dot(matches, chosen, preferred_element_type=F32)

    self_units = pool[me].astype(F32).T

    for k in range(1, stages):
        exchange_arrival(k, *out_group).wait_recv()
    rows = jnp.concatenate([out_recv[s] for s in range(stages)], axis=0).astype(F32)
    radius = jnp.sqrt(jnp.sum(rows * rows, axis=0, keepdims=True) + EPSILON)
    unit_rows = rows / radius
    anchors = unit_rows.astype(BF16)
    positive = jnp.exp(jnp.sum(anchors.astype(F32) * self_units, axis=0, keepdims=True) * INVERSE_TEMP)

    for k in range(chips):
        pass_arrival(k).wait_recv()

    totals = positive
    numerator = jnp.zeros((segment, depth), F32)
    for q in range(records):
        units = pool[q]
        allowed = jnp.where(ids_ref[q] != ids_ref[me], 1.0, 0.0).astype(F32)
        scores = jnp.dot(units, anchors, preferred_element_type=F32) * INVERSE_TEMP
        weights = counts[q * segment : (q + 1) * segment, :] * allowed * jnp.exp(scores)
        totals += jnp.sum(weights, axis=0, keepdims=True)
        numerator += jnp.dot(weights.T.astype(BF16), units, preferred_element_type=F32)
    anchor_grad = ((positive / totals - 1.0) * self_units + numerator.T / totals) * (
        INVERSE_TEMP * LOSS_SCALE
    )
    frame_grad = (
        anchor_grad - unit_rows * jnp.sum(unit_rows * anchor_grad, axis=0, keepdims=True)
    ) / radius
    for s in range(stages):
        back_send[s] = frame_grad[s * channels : (s + 1) * channels, :].astype(BF16)
    for k in range(1, stages):
        exchange(k, *back_group).start()
    back_recv[here] = back_send[here]
    for k in range(1, stages):
        exchange_arrival(k, *back_group).wait_recv()

    cotangent = jnp.concatenate([back_recv[s] for s in range(stages)], axis=1).astype(F32)
    second_out[0] = (cotangent * mixed_two[...]).astype(BF16)
    late_drive = cotangent * second_ref[0].astype(F32)
    spec = forward((late_drive.astype(BF16), None))

    shard = channels // records

    def spread(which, update):
        for r in range(records):
            reduce_send[which, r] = update[r * shard : (r + 1) * shard, :].astype(BF16)
        for k in range(1, records):
            peer = lax.rem(me + k, records)
            remote(
                reduce_send.at[which, peer], reduce_recv.at[which, me],
                reduce_send_sem.at[which, k], reduce_recv_sem.at[which, k], (peer, here),
            ).start()

    def share(which, target):
        for k in range(1, records):
            peer = lax.rem(me + records - k, records)
            remote(
                reduce_send.at[which, peer], reduce_recv.at[which, peer],
                reduce_send_sem.at[which, k], reduce_recv_sem.at[which, k], (peer, here),
            ).wait_recv()
        total = reduce_send[which, me].astype(F32)
        for k in range(1, records):
            total += reduce_recv[which, lax.rem(me + records - k, records)].astype(F32)
        target[me] = total.astype(BF16)
        for k in range(1, records):
            peer = lax.rem(me + k, records)
            remote(
                target.at[me], target.at[me],
                share_send_sem.at[which, k], share_recv_sem.at[which, k], (peer, here),
            ).start()

    spread(1, correlated(spec, hidden_spec, fine=False))
    hidden_grad = correlated(spec, late_spec) + late_skip * late_drive
    first_out[0] = (hidden_grad * mixed_one[...]).astype(BF16)
    early_drive = hidden_grad * first_ref[0].astype(F32)
    spec = forward((early_drive.astype(BF16), None))
    share(1, late_out)
    spread(0, correlated(spec, signal_spec, fine=False))
    values_out[0] = (correlated(spec, early_spec) + early_skip * early_drive).astype(BF16)
    share(0, early_out)

    for k in range(1, chips):
        pool_copy(k).wait_send()
    for k in range(chips):
        pass_copy(k).wait_send()
    for k in range(1, stages):
        exchange(k, *out_group).wait_send()
        exchange(k, *back_group).wait_send()
    for which, target in ((1, late_out), (0, early_out)):
        for k in range(1, records):
            peer = lax.rem(me + k, records)
            remote(
                reduce_send.at[which, peer], reduce_recv.at[which, me],
                reduce_send_sem.at[which, k], reduce_recv_sem.at[which, k], (peer, here),
            ).wait_send()
            source = lax.rem(me + records - k, records)
            shared = remote(
                target.at[source], target.at[source],
                share_send_sem.at[which, k], share_recv_sem.at[which, k], (source, here),
            )
            shared.wait_recv()
            shared.wait_send()


def finish(frames, *refs):
    for source, target in zip(refs[:3], refs[5:8]):
        target[...] = source[...]
    for source, target in zip(refs[3:5], refs[8:]):
        target[...] = source[...].astype(F32) / frames


def local(
    records, stages,
    values, gates_first, gates_second, filter_early, filter_late, skip_early, skip_late,
    targets, negative_rows, recording_ids,
):
    _, channels, frames = values.shape
    _, segment, depth = targets.shape
    if 8 * frames * frames > TABLE_BYTES:
        return local_large(
            values, gates_first, gates_second, filter_early, filter_late, skip_early, skip_late,
            targets, negative_rows, recording_ids,
        )
    high, low, turn = tables(frames)
    shard = channels // records
    vmem = pl.BlockSpec(memory_space=pltpu.VMEM)
    stream = jax.ShapeDtypeStruct(values.shape, BF16)
    update = jax.ShapeDtypeStruct((records, shard, frames), BF16)
    exchange = pltpu.VMEM((stages, channels, segment), BF16)
    reduce = pltpu.VMEM((2, records, shard, frames), BF16)
    plane = pltpu.VMEM((channels, frames), F32)
    spec = pltpu.VMEM((2, channels, frames), F32)
    semaphores = pltpu.SemaphoreType.DMA
    chips = records // 2
    results = pl.pallas_call(
        functools.partial(kernel, (records, stages)),
        out_shape=(stream, stream, stream, update, update),
        in_specs=[vmem] * 9 + [pl.BlockSpec(memory_space=pltpu.SMEM)] + [vmem] * 3,
        out_specs=(vmem,) * 5,
        scratch_shapes=[
            pltpu.VMEM((records, segment, depth), BF16),
            exchange, exchange, exchange, exchange, reduce, reduce,
            plane, plane, spec, spec, spec, spec,
            semaphores((chips,)), semaphores((chips,)), semaphores((chips,)), semaphores((chips,)),
            semaphores((stages,)), semaphores((stages,)), semaphores((stages,)), semaphores((stages,)),
            semaphores((2, records)), semaphores((2, records)),
            semaphores((2, records)), semaphores((2, records)),
        ],
        compiler_params=pltpu.CompilerParams(
            collective_id=0, has_side_effects=True, vmem_limit_bytes=63 * 1024 * 1024
        ),
    )(
        values, gates_first, gates_second, filter_early, filter_late,
        skip_early[None], skip_late[None], targets, negative_rows, recording_ids,
        jnp.asarray(high), jnp.asarray(low), jnp.asarray(turn),
    )
    wide = jax.ShapeDtypeStruct(update.shape, F32)
    *streams, early, late = pl.pallas_call(
        functools.partial(finish, frames),
        out_shape=(stream, stream, stream, wide, wide),
        in_specs=[vmem] * 5,
        out_specs=(vmem,) * 5,
        compiler_params=pltpu.CompilerParams(vmem_limit_bytes=63 * 1024 * 1024),
    )(*results)
    return (*streams, early.reshape(channels, frames), late.reshape(channels, frames))


def solution(mesh):
    placed = (
        P("dp", "seq", None),
        P("dp", "seq", None),
        P("dp", "seq", None),
        P("seq", None),
        P("seq", None),
        P("seq"),
        P("seq"),
        P("dp", "seq", None),
        P("dp", "seq", None),
        P(),
    )
    return jax.shard_map(
        functools.partial(local, mesh.shape["dp"], mesh.shape["seq"]),
        mesh=mesh,
        in_specs=placed,
        out_specs=(
            P("dp", "seq", None),
            P("dp", "seq", None),
            P("dp", "seq", None),
            P("seq", None),
            P("seq", None),
        ),
        check_vma=False,
    )
```

profile of v0, /device:TPU:0, one launch (start us, length us, event | category | flops | bytes accessed | tf_op | source)
XLA Modules:
  0.0 54.9 jit_solution(16579394937938432914)
XLA Ops:
  0.6 51.7 %shard_map.164 = (bf16[1,256,512]{2,1,0:T(8,128)(2,1)}, bf16[1,256,512]{2,1,0:T(8,128)(2,1)}, bf16[1,256,512]{2,1,0:T(8,128)(2,1)}, bf16[8,32,512]{2,1,0:T(8,128)(2,1)}, bf16[8,32,512]{2,1,0:T(8,128)(2,1)}) custom-call(bf16[1,256,512]{2,1,0:T(8,128)(2,1)} %values_ref.1, bf16[1,256,512]{2,1,0:T(8,128)(2,1)} %first_ref.1, bf16[1,256,512]{2,1,0:T(8,128)(2,1)} %second_ref.1, ...), custom_call_target="tpu_custom_call" | custom-call | tf_op jit(solution)/shard_map/pallas_call | solution.py:552
  52.4 2.5 %shard_map.165 = (bf16[1,256,512]{2,1,0:T(8,128)(2,1)}, bf16[1,256,512]{2,1,0:T(8,128)(2,1)}, bf16[1,256,512]{2,1,0:T(8,128)(2,1)}, f32[8,32,512]{2,1,0:T(8,128)}, f32[8,32,512]{2,1,0:T(8,128)}) custom-call(bf16[1,256,512]{2,1,0:T(8,128)(2,1)} %get-tuple-element.15.refs_0_, bf16[1,256,512]{2,1,0:T(8,128)(2,1)} %get-tuple-element.16.refs_1_, ...), custom_call_target="tpu_custom_call" | custom-call | tf_op jit(solution)/shard_map/pallas_call | solution.py:575
where the time goes:
time: 55 us; the launch traced here: 54.9 us
  Pallas kernels  54.2 us (99%)
  between operations  0.64 us (1%)
    pallas_call x1, Pallas kernels, local(): pl.pallas_call(functools.partial(kernel, (records, stages)), out_shape=(s...  51.7 us
    pallas_call x1, Pallas kernels, local(): pl.pallas_call(functools.partial(finish, frames), out_shape=(stream, stre...  2.51 us

commit v1 on v0

--- a/solution.py
+++ b/solution.py
@@ -17,6 +17,8 @@
 BF16 = jnp.bfloat16
 TABLE_BYTES = 16 * 1024 * 1024
 INNER_WIDTH = 128
+GRID_CHIPS = 4
+VMEM_BYTES = 40 * 1024 * 1024
 HIGHEST = lax.Precision.HIGHEST
 
 
@@ -268,34 +270,60 @@
 
 def kernel(
     sizes,
+    values_hbm, first_hbm, second_hbm, early_hbm, late_hbm, early_skip_hbm, late_skip_hbm,
+    targets_hbm, rows_hbm, ids_hbm, high_hbm, low_hbm, turn_hbm,
+    values_out, first_out, second_out, early_out, late_out,
     values_ref, first_ref, second_ref, early_ref, late_ref, early_skip_ref, late_skip_ref,
     targets_ref, rows_ref, ids_ref, high_ref, low_ref, turn_ref,
-    values_out, first_out, second_out, early_out, late_out,
-    pool, out_send, out_recv, back_send, back_recv, reduce_send, reduce_recv,
-    mixed_one, mixed_two, early_spec, late_spec, signal_spec, hidden_spec,
-    pool_send_sem, pool_recv_sem, pass_send_sem, pass_recv_sem,
+    pool, out_send, out_recv, back_send, back_recv, pair_send, pair_recv, ring_send, ring_recv,
+    mixed_one, mixed_two, early_spec, late_spec, signal_spec, hidden_spec, counts_ref,
+    load_sem, pool_send_sem, pool_recv_sem, pass_send_sem, pass_recv_sem,
     out_send_sem, out_recv_sem, back_send_sem, back_recv_sem,
-    reduce_send_sem, reduce_recv_sem, share_send_sem, share_recv_sem,
+    pair_send_sem, pair_recv_sem, ring_send_sem, ring_recv_sem,
+    share_send_sem, share_recv_sem, last_send_sem, last_recv_sem,
 ):
     records, stages = sizes
     chips = records // 2
     me = lax.axis_index("dp")
     here = lax.axis_index("seq")
     chip, core = me // 2, me % 2
+    across, along = chip % 2, chip // 2
     partner = chip * 2 + (1 - core)
+    x_chip = along * 2 + (1 - across)
+    y_chip = (1 - along) * 2 + across
+    d_chip = (1 - along) * 2 + (1 - across)
+    near = (x_chip, y_chip, d_chip)
     channels, frames = mixed_one.shape
     segment = pool.shape[1]
     depth = pool.shape[2]
+    part = segment // 2
 
     barrier = pltpu.get_barrier_semaphore()
-    for k in range(1, records):
-        pl.semaphore_signal(
-            barrier, inc=1, device_id=(lax.rem(me + k, records), here), device_id_type=MESH
-        )
-    for k in range(1, stages):
-        pl.semaphore_signal(
-            barrier, inc=1, device_id=(me, lax.rem(here + k, stages)), device_id_type=MESH
-        )
+    peers = [(partner, here)] + [(c * 2 + core, here) for c in near]
+    peers += [(me, lax.rem(here + k, stages)) for k in range(1, stages)]
+    for peer in peers:
+        pl.semaphore_signal(barrier, inc=1, device_id=peer, device_id_type=MESH)
+
+    loads = {
+        name: pltpu.make_async_copy(source, target, load_sem.at[i])
+        for i, (name, source, target) in enumerate((
+            ("targets", targets_hbm.at[0], targets_ref),
+            ("early", early_hbm, early_ref),
+            ("high", high_hbm, high_ref),
+            ("low", low_hbm, low_ref),
+            ("late", late_hbm, late_ref),
+            ("turn", turn_hbm, turn_ref),
+            ("values", values_hbm.at[0], values_ref),
+            ("first", first_hbm.at[0], first_ref),
+            ("second", second_hbm.at[0], second_ref),
+            ("early_skip", early_skip_hbm, early_skip_ref),
+            ("late_skip", late_skip_hbm, late_skip_ref),
+            ("rows", rows_hbm.at[0], rows_ref),
+            ("ids", ids_hbm, ids_ref),
+        ))
+    }
+    for load in loads.values():
+        load.start()
 
     def remote(source, target, send, recv, device):
         return pltpu.make_async_remote_copy(
@@ -303,36 +331,54 @@
             device_id=device, device_id_type=MESH,
         )
 
-    full = targets_ref[0].astype(F32)
+    loads["targets"].wait()
+    full = targets_ref[...].astype(F32)
     norm = jnp.sqrt(jnp.sum(full * full, axis=-1, keepdims=True) + EPSILON)
     pool[me] = (full / norm).astype(BF16)
-    pl.semaphore_wait(barrier, records + stages - 2)
-
-    def pool_copy(k):
-        peer = lax.rem(chip + k, chips) * 2 + core
-        return remote(pool.at[me], pool.at[me], pool_send_sem.at[k], pool_recv_sem.at[k], (peer, here))
-
-    def pool_arrival(k):
-        slot = lax.rem(chip + chips - k, chips) * 2 + core
-        return slot, remote(
-            pool.at[slot], pool.at[slot], pool_send_sem.at[k], pool_recv_sem.at[k], (slot, here)
-        )
-
-    def pass_copy(k):
-        slot = lax.rem(chip + chips - k, chips) * 2 + core
+    pl.semaphore_wait(barrier, len(peers))
+
+    def piece(owner, h):
+        return pool.at[owner * 2 + core, pl.ds(h * part, part)]
+
+    def pool_copy(n):
+        owner, h, to = (
+            (chip, 1, x_chip), (chip, 0, y_chip), (chip, 0, x_chip), (chip, 1, y_chip),
+            (y_chip, 0, x_chip), (x_chip, 1, y_chip),
+        )[n]
+        block = piece(owner, h)
         return remote(
-            pool.at[slot], pool.at[slot], pass_send_sem.at[k], pass_recv_sem.at[k], (partner, here)
-        )
-
-    def pass_arrival(k):
-        slot = lax.rem(chip + chips - k, chips) * 2 + (1 - core)
+            block, block, pool_send_sem.at[n], pool_recv_sem.at[n], (to * 2 + core, here)
+        )
+
+    def pool_arrival(n):
+        owner, h, to = (
+            (x_chip, 1, x_chip), (y_chip, 0, y_chip), (x_chip, 0, x_chip), (y_chip, 1, y_chip),
+            (d_chip, 0, x_chip), (d_chip, 1, y_chip),
+        )[n]
+        block = piece(owner, h)
         return remote(
-            pool.at[slot], pool.at[slot], pass_send_sem.at[k], pass_recv_sem.at[k], (partner, here)
-        )
-
-    for k in range(1, chips):
-        pool_copy(k).start()
-    pass_copy(0).start()
+            block, block, pool_send_sem.at[n], pool_recv_sem.at[n], (to * 2 + core, here)
+        )
+
+    def passed(n, lane):
+        if n == 6:
+            block = pool.at[chip * 2 + lane]
+        else:
+            owner, h = (
+                (x_chip, 1), (y_chip, 0), (x_chip, 0), (y_chip, 1), (d_chip, 0), (d_chip, 1)
+            )[n]
+            block = pool.at[owner * 2 + lane, pl.ds(h * part, part)]
+        return remote(block, block, pass_send_sem.at[n], pass_recv_sem.at[n], (partner, here))
+
+    def pass_copy(n):
+        return passed(n, core)
+
+    def pass_arrival(n):
+        return passed(n, 1 - core)
+
+    for n in range(4):
+        pool_copy(n).start()
+    pass_copy(6).start()
 
     def forward(parts):
         return tuple(product(parts, high_ref[i], low_ref[i]) for i in (0, 1))
@@ -368,19 +414,25 @@
     def column(row):
         return jnp.broadcast_to(row, (8, channels)).T[:, 0:1]
 
+    for name in ("early", "high", "low", "turn"):
+        loads[name].wait()
+    keep(early_spec, unshifted(forward(halves(early_ref[...]))))
+    loads["late"].wait()
+    keep(late_spec, unshifted(forward(halves(late_ref[...]))))
+    for name in ("values", "early_skip", "late_skip"):
+        loads[name].wait()
     early_skip = column(early_skip_ref[...])
     late_skip = column(late_skip_ref[...])
-
-    keep(early_spec, unshifted(forward(halves(early_ref[...]))))
-    keep(late_spec, unshifted(forward(halves(late_ref[...]))))
-    spec = forward((values_ref[0], None))
-    mixed_one[...] = convolved(spec, early_spec) + early_skip * values_ref[0].astype(F32)
+    spec = forward((values_ref[...], None))
+    mixed_one[...] = convolved(spec, early_spec) + early_skip * values_ref[...].astype(F32)
     signal_waves = spec
-    hidden = first_ref[0].astype(F32) * mixed_one[...]
+    loads["first"].wait()
+    hidden = first_ref[...].astype(F32) * mixed_one[...]
     spec = forward((hidden.astype(BF16), None))
     mixed_two[...] = convolved(spec, late_spec) + late_skip * hidden
 
-    output = second_ref[0].astype(F32) * mixed_two[...]
+    loads["second"].wait()
+    output = second_ref[...].astype(F32) * mixed_two[...]
     for s in range(stages):
         out_send[s] = output[:, s * segment : (s + 1) * segment].astype(BF16)
 
@@ -397,25 +449,37 @@
     for k in range(1, stages):
         exchange(k, *out_group).start()
     out_recv[here] = out_send[here]
+
+    pool_arrival(1).wait_recv()
+    pool_copy(4).start()
+    pass_copy(1).start()
+    pool_arrival(0).wait_recv()
+    pool_copy(5).start()
+    pass_copy(0).start()
+
     keep(signal_spec, unshifted(signal_waves))
     keep(hidden_spec, unshifted(spec))
 
-    for k in range(1, chips):
-        pool_arrival(k)[1].wait_recv()
-        pass_copy(k).start()
-
-    blocks = rows_ref.shape[1]
-    draws = rows_ref.shape[2]
+    loads["rows"].wait()
+    loads["ids"].wait()
+    blocks = rows_ref.shape[0]
+    draws = rows_ref.shape[1]
     block_size = segment // blocks
     frame_block = lax.broadcasted_iota(jnp.int32, (draws, segment), 1) // block_size
     counts = jnp.zeros((records * segment, segment), F32)
     position = lax.broadcasted_iota(jnp.int32, (records * segment, draws), 0)
     for b in range(blocks):
-        matches = jnp.where(position == rows_ref[0, b : b + 1, :], 1.0, 0.0).astype(BF16)
+        matches = jnp.where(position == rows_ref[b : b + 1, :], 1.0, 0.0).astype(BF16)
         chosen = jnp.where(frame_block == b, 1.0, 0.0).astype(BF16)
         counts += jnp.dot(matches, chosen, preferred_element_type=F32)
+    for c in range(chips):
+        counts_ref[c] = counts[c * 2 * segment : (c + 1) * 2 * segment, :]
 
     self_units = pool[me].astype(F32).T
+
+    for n in (2, 3):
+        pool_arrival(n).wait_recv()
+        pass_copy(n).start()
 
     for k in range(1, stages):
         exchange_arrival(k, *out_group).wait_recv()
@@ -425,18 +489,32 @@
     anchors = unit_rows.astype(BF16)
     positive = jnp.exp(jnp.sum(anchors.astype(F32) * self_units, axis=0, keepdims=True) * INVERSE_TEMP)
 
-    for k in range(chips):
-        pass_arrival(k).wait_recv()
-
-    totals = positive
-    numerator = jnp.zeros((segment, depth), F32)
-    for q in range(records):
-        units = pool[q]
-        allowed = jnp.where(ids_ref[q] != ids_ref[me], 1.0, 0.0).astype(F32)
+    upper = lax.broadcasted_iota(jnp.int32, (2 * segment, 1), 0) < segment
+
+    def against(c):
+        units = pool[pl.ds(c * 2, 2)].reshape(2 * segment, depth)
+        own_id = ids_ref[me]
+        allowed = [jnp.where(ids_ref[c * 2 + i] != own_id, 1.0, 0.0).astype(F32) for i in (0, 1)]
         scores = jnp.dot(units, anchors, preferred_element_type=F32) * INVERSE_TEMP
-        weights = counts[q * segment : (q + 1) * segment, :] * allowed * jnp.exp(scores)
-        totals += jnp.sum(weights, axis=0, keepdims=True)
-        numerator += jnp.dot(weights.T.astype(BF16), units, preferred_element_type=F32)
+        weights = counts_ref[c] * jnp.where(upper, allowed[0], allowed[1]) * jnp.exp(scores)
+        return (
+            jnp.sum(weights, axis=0, keepdims=True),
+            jnp.dot(weights.T.astype(BF16), units, preferred_element_type=F32),
+        )
+
+    pass_arrival(6).wait_recv()
+    summed, numerator = against(chip)
+    totals = positive + summed
+    for c, pieces in ((x_chip, (0, 2)), (y_chip, (1, 3)), (d_chip, (4, 5))):
+        if pieces == (4, 5):
+            for n in pieces:
+                pool_arrival(n).wait_recv()
+                pass_copy(n).start()
+        for n in pieces:
+            pass_arrival(n).wait_recv()
+        summed, partial = against(c)
+        totals += summed
+        numerator += partial
     anchor_grad = ((positive / totals - 1.0) * self_units + numerator.T / totals) * (
         INVERSE_TEMP * LOSS_SCALE
     )
@@ -451,79 +529,131 @@
     for k in range(1, stages):
         exchange_arrival(k, *back_group).wait_recv()
 
+    half = channels // 2
+    shard = half // chips
+
+    def pair_copy(which, lane):
+        return remote(
+            pair_send.at[which, lane], pair_recv.at[which],
+            pair_send_sem.at[which], pair_recv_sem.at[which], (partner, here),
+        )
+
+    def spread(which, update):
+        for i in (0, 1):
+            pair_send[which, i] = update[i * half : (i + 1) * half, :].astype(BF16)
+        pair_copy(which, 1 - core).start()
+
+    def ring_copy(which, n):
+        return remote(
+            ring_send.at[which, near[n]], ring_recv.at[which, n],
+            ring_send_sem.at[which, n], ring_recv_sem.at[which, n], (near[n] * 2 + core, here),
+        )
+
+    def gather(which):
+        pair_copy(which, core).wait_recv()
+        joined = pair_send[which, core].astype(F32) + pair_recv[which].astype(F32)
+        for j in range(chips):
+            ring_send[which, j] = joined[j * shard : (j + 1) * shard, :].astype(BF16)
+        for n in (2, 0, 1):
+            ring_copy(which, n).start()
+
+    def share_copy(which, target, n):
+        block = target.at[core * chips + chip]
+        return remote(
+            block, block, share_send_sem.at[which, n], share_recv_sem.at[which, n],
+            (near[n] * 2 + core, here),
+        )
+
+    def share_arrival(which, target, n):
+        block = target.at[core * chips + near[n]]
+        return remote(
+            block, block, share_send_sem.at[which, n], share_recv_sem.at[which, n],
+            (near[n] * 2 + core, here),
+        )
+
+    sources = near + (chip,)
+
+    def last_copy(which, target, n):
+        block = target.at[core * chips + sources[n]]
+        return remote(
+            block, block, last_send_sem.at[which, n], last_recv_sem.at[which, n], (partner, here)
+        )
+
+    def last_arrival(which, target, n):
+        block = target.at[(1 - core) * chips + sources[n]]
+        return remote(
+            block, block, last_send_sem.at[which, n], last_recv_sem.at[which, n], (partner, here)
+        )
+
+    def share(which, target):
+        total = ring_send[which, chip].astype(F32)
+        for n in range(3):
+            ring_copy(which, n).wait_recv()
+            total += ring_recv[which, n].astype(F32)
+        target[core * chips + chip] = total.astype(BF16)
+        for n in (2, 0, 1):
+            share_copy(which, target, n).start()
+        last_copy(which, target, 3).start()
+
+    def relay(which, target):
+        for n in range(3):
+            share_arrival(which, target, n).wait_recv()
+            last_copy(which, target, n).start()
+
     cotangent = jnp.concatenate([back_recv[s] for s in range(stages)], axis=1).astype(F32)
+    late_drive = cotangent * second_ref[...].astype(F32)
+    spec = forward((late_drive.astype(BF16), None))
+    hidden_grad = correlated(spec, late_spec) + late_skip * late_drive
+    spread(1, correlated(spec, hidden_spec, fine=False))
+    early_drive = hidden_grad * first_ref[...].astype(F32)
+    spec = forward((early_drive.astype(BF16), None))
+    spread(0, correlated(spec, signal_spec, fine=False))
+    gather(1)
     second_out[0] = (cotangent * mixed_two[...]).astype(BF16)
-    late_drive = cotangent * second_ref[0].astype(F32)
-    spec = forward((late_drive.astype(BF16), None))
-
-    shard = channels // records
-
-    def spread(which, update):
-        for r in range(records):
-            reduce_send[which, r] = update[r * shard : (r + 1) * shard, :].astype(BF16)
-        for k in range(1, records):
-            peer = lax.rem(me + k, records)
-            remote(
-                reduce_send.at[which, peer], reduce_recv.at[which, me],
-                reduce_send_sem.at[which, k], reduce_recv_sem.at[which, k], (peer, here),
-            ).start()
-
-    def share(which, target):
-        for k in range(1, records):
-            peer = lax.rem(me + records - k, records)
-            remote(
-                reduce_send.at[which, peer], reduce_recv.at[which, peer],
-                reduce_send_sem.at[which, k], reduce_recv_sem.at[which, k], (peer, here),
-            ).wait_recv()
-        total = reduce_send[which, me].astype(F32)
-        for k in range(1, records):
-            total += reduce_recv[which, lax.rem(me + records - k, records)].astype(F32)
-        target[me] = total.astype(BF16)
-        for k in range(1, records):
-            peer = lax.rem(me + k, records)
-            remote(
-                target.at[me], target.at[me],
-                share_send_sem.at[which, k], share_recv_sem.at[which, k], (peer, here),
-            ).start()
-
-    spread(1, correlated(spec, hidden_spec, fine=False))
-    hidden_grad = correlated(spec, late_spec) + late_skip * late_drive
     first_out[0] = (hidden_grad * mixed_one[...]).astype(BF16)
-    early_drive = hidden_grad * first_ref[0].astype(F32)
-    spec = forward((early_drive.astype(BF16), None))
+    gather(0)
+    values_out[0] = (correlated(spec, early_spec) + early_skip * early_drive).astype(BF16)
     share(1, late_out)
-    spread(0, correlated(spec, signal_spec, fine=False))
-    values_out[0] = (correlated(spec, early_spec) + early_skip * early_drive).astype(BF16)
     share(0, early_out)
-
-    for k in range(1, chips):
-        pool_copy(k).wait_send()
-    for k in range(chips):
-        pass_copy(k).wait_send()
+    relay(1, late_out)
+    relay(0, early_out)
+
+    for n in range(6):
+        pool_copy(n).wait_send()
+    for n in range(7):
+        pass_copy(n).wait_send()
     for k in range(1, stages):
         exchange(k, *out_group).wait_send()
         exchange(k, *back_group).wait_send()
     for which, target in ((1, late_out), (0, early_out)):
-        for k in range(1, records):
-            peer = lax.rem(me + k, records)
-            remote(
-                reduce_send.at[which, peer], reduce_recv.at[which, me],
-                reduce_send_sem.at[which, k], reduce_recv_sem.at[which, k], (peer, here),
-            ).wait_send()
-            source = lax.rem(me + records - k, records)
-            shared = remote(
-                target.at[source], target.at[source],
-                share_send_sem.at[which, k], share_recv_sem.at[which, k], (source, here),
-            )
-            shared.wait_recv()
-            shared.wait_send()
-
-
-def finish(frames, *refs):
-    for source, target in zip(refs[:3], refs[5:8]):
-        target[...] = source[...]
-    for source, target in zip(refs[3:5], refs[8:]):
-        target[...] = source[...].astype(F32) / frames
+        pair_copy(which, 1 - core).wait_send()
+        for n in range(3):
+            ring_copy(which, n).wait_send()
+            share_copy(which, target, n).wait_send()
+        for n in range(4):
+            last_copy(which, target, n).wait_send()
+            last_arrival(which, target, n).wait_recv()
+
+
+def finish(
+    frames, values_in, first_in, second_in, early_in, late_in,
+    values_out, first_out, second_out, early_out, late_out, early_wide, late_wide, sems,
+):
+    copies = [
+        pltpu.make_async_copy(source, target, sems.at[i])
+        for i, (source, target) in enumerate((
+            (values_in, values_out), (first_in, first_out), (second_in, second_out),
+            (early_wide, early_out), (late_wide, late_out),
+        ))
+    ]
+    for copy in copies[:3]:
+        copy.start()
+    late_wide[...] = late_in[...].astype(F32) / frames
+    copies[4].start()
+    early_wide[...] = early_in[...].astype(F32) / frames
+    copies[3].start()
+    for copy in copies:
+        copy.wait()
 
 
 def local(
@@ -533,51 +663,66 @@
 ):
     _, channels, frames = values.shape
     _, segment, depth = targets.shape
-    if 8 * frames * frames > TABLE_BYTES:
+    if 8 * frames * frames > TABLE_BYTES or records != 2 * GRID_CHIPS:
         return local_large(
             values, gates_first, gates_second, filter_early, filter_late, skip_early, skip_late,
             targets, negative_rows, recording_ids,
         )
     high, low, turn = tables(frames)
-    shard = channels // records
+    chips = records // 2
+    half = channels // 2
+    shard = half // chips
+    blocks, draws = negative_rows.shape[1:]
     vmem = pl.BlockSpec(memory_space=pltpu.VMEM)
-    stream = jax.ShapeDtypeStruct(values.shape, BF16)
-    update = jax.ShapeDtypeStruct((records, shard, frames), BF16)
+    hbm = pl.BlockSpec(memory_space=pltpu.HBM)
+    stream = pltpu.VMEM(values.shape, BF16)
+    update = pltpu.VMEM((records, shard, frames), BF16)
     exchange = pltpu.VMEM((stages, channels, segment), BF16)
-    reduce = pltpu.VMEM((2, records, shard, frames), BF16)
     plane = pltpu.VMEM((channels, frames), F32)
+    narrow = pltpu.VMEM((channels, frames), BF16)
     spec = pltpu.VMEM((2, channels, frames), F32)
+    skip = pltpu.VMEM((1, channels), F32)
+    table = pltpu.VMEM(high.shape, BF16)
     semaphores = pltpu.SemaphoreType.DMA
-    chips = records // 2
     results = pl.pallas_call(
         functools.partial(kernel, (records, stages)),
         out_shape=(stream, stream, stream, update, update),
-        in_specs=[vmem] * 9 + [pl.BlockSpec(memory_space=pltpu.SMEM)] + [vmem] * 3,
+        in_specs=[hbm] * 13,
         out_specs=(vmem,) * 5,
         scratch_shapes=[
+            narrow, narrow, narrow, plane, plane, skip, skip,
+            pltpu.VMEM((segment, depth), BF16), pltpu.VMEM((blocks, draws), jnp.int32),
+            pltpu.SMEM((records,), jnp.int32), table, table, pltpu.VMEM(turn.shape, F32),
             pltpu.VMEM((records, segment, depth), BF16),
-            exchange, exchange, exchange, exchange, reduce, reduce,
+            exchange, exchange, exchange, exchange,
+            pltpu.VMEM((2, 2, half, frames), BF16), pltpu.VMEM((2, half, frames), BF16),
+            pltpu.VMEM((2, chips, shard, frames), BF16), pltpu.VMEM((2, 3, shard, frames), BF16),
             plane, plane, spec, spec, spec, spec,
-            semaphores((chips,)), semaphores((chips,)), semaphores((chips,)), semaphores((chips,)),
+            pltpu.VMEM((chips, 2 * segment, segment), F32),
+            semaphores((13,)), semaphores((6,)), semaphores((6,)), semaphores((7,)), semaphores((7,)),
             semaphores((stages,)), semaphores((stages,)), semaphores((stages,)), semaphores((stages,)),
-            semaphores((2, records)), semaphores((2, records)),
-            semaphores((2, records)), semaphores((2, records)),
+            semaphores((2,)), semaphores((2,)), semaphores((2, 3)), semaphores((2, 3)),
+            semaphores((2, 3)), semaphores((2, 3)), semaphores((2, 4)), semaphores((2, 4)),
         ],
         compiler_params=pltpu.CompilerParams(
-            collective_id=0, has_side_effects=True, vmem_limit_bytes=63 * 1024 * 1024
+            collective_id=0, has_side_effects=True, vmem_limit_bytes=VMEM_BYTES
         ),
-    )(
-        values, gates_first, gates_second, filter_early, filter_late,
-        skip_early[None], skip_late[None], targets, negative_rows, recording_ids,
-        jnp.asarray(high), jnp.asarray(low), jnp.asarray(turn),
-    )
-    wide = jax.ShapeDtypeStruct(update.shape, F32)
+    )(*(
+        pltpu.with_memory_space_constraint(operand, pltpu.HBM)
+        for operand in (
+            values, gates_first, gates_second, filter_early, filter_late,
+            skip_early[None], skip_late[None], targets, negative_rows, recording_ids,
+            jnp.asarray(high), jnp.asarray(low), jnp.asarray(turn),
+        )
+    ))
+    wide = (records, shard, frames)
     *streams, early, late = pl.pallas_call(
         functools.partial(finish, frames),
-        out_shape=(stream, stream, stream, wide, wide),
+        out_shape=(jax.ShapeDtypeStruct(values.shape, BF16),) * 3 + (jax.ShapeDtypeStruct(wide, F32),) * 2,
         in_specs=[vmem] * 5,
-        out_specs=(vmem,) * 5,
-        compiler_params=pltpu.CompilerParams(vmem_limit_bytes=63 * 1024 * 1024),
+        out_specs=(hbm,) * 5,
+        scratch_shapes=[pltpu.VMEM(wide, F32), pltpu.VMEM(wide, F32), semaphores((5,))],
+        compiler_params=pltpu.CompilerParams(vmem_limit_bytes=VMEM_BYTES),
     )(*results)
     return (*streams, early.reshape(channels, frames), late.reshape(channels, frames))
 

time: 55 us -> 42.4 us (0.77)
  Pallas kernels: 54.2 us -> 41.6 us
    pallas_call x1, Pallas kernels: 51.7 us -> 40.3 us  [local(): pl.pallas_call(functools.partial(kernel, (records, stages)), out_shape=(s...]
    pallas_call x1, Pallas kernels: 2.51 us -> 1.27 us  [local(): pl.pallas_call(functools.partial(finish, frames), out_shape=(jax.ShapeDty...]
where the time goes in v1:
time: 42.4 us; the launch traced here: 42.2 us
  Pallas kernels  41.6 us (98%)
  between operations  0.64 us (2%)
    pallas_call x1, Pallas kernels, local(): pl.pallas_call(functools.partial(kernel, (records, stages)), out_shape=(s...  40.3 us
    pallas_call x1, Pallas kernels, local(): pl.pallas_call(functools.partial(finish, frames), out_shape=(jax.ShapeDty...  1.27 us

profile of v1, /device:TPU:0, one launch (start us, length us, event | category | flops | bytes accessed | tf_op | source)
XLA Modules:
  0.0 42.2 jit_solution(6346916206856555245)
XLA Ops:
  0.6 40.3 %shard_map.164 = (bf16[1,256,512]{2,1,0:T(8,128)(2,1)S(1)}, bf16[1,256,512]{2,1,0:T(8,128)(2,1)S(1)}, bf16[1,256,512]{2,1,0:T(8,128)(2,1)S(1)}, bf16[8,32,512]{2,1,0:T(8,128)(2,1)S(1)}, bf16[8,32,512]{2,1,0:T(8,128)(2,1)S(1)}) custom-call(bf16[1,256,512]{2,1,0:T(8,128)(2,1)} %values_hbm.1, bf16[1,256,512]{2,1,0:T(8,128)(2,1)} %first_hbm.1, ...), custom_call_target="tpu_custom_call" | custom-call | tf_op jit(solution)/shard_map/pallas_call | solution.py:687
  41.0 1.3 %shard_map.165 = (bf16[1,256,512]{2,1,0:T(8,128)(2,1)}, bf16[1,256,512]{2,1,0:T(8,128)(2,1)}, bf16[1,256,512]{2,1,0:T(8,128)(2,1)}, f32[8,32,512]{2,1,0:T(8,128)}, f32[8,32,512]{2,1,0:T(8,128)}) custom-call(bf16[1,256,512]{2,1,0:T(8,128)(2,1)S(1)} %get-tuple-element.15.values_in, bf16[1,256,512]{2,1,0:T(8,128)(2,1)S(1)} %get-tuple-element.16.first_in, ...), custom_call_target="tpu_custom_call" | custom-call | tf_op jit(solution)/shard_map/pallas_call | solution.py:719

commit v2 on v1

--- a/solution.py
+++ b/solution.py
@@ -18,6 +18,7 @@
 TABLE_BYTES = 16 * 1024 * 1024
 INNER_WIDTH = 128
 GRID_CHIPS = 4
+CHUNKS = 2
 VMEM_BYTES = 40 * 1024 * 1024
 HIGHEST = lax.Precision.HIGHEST
 
@@ -241,41 +242,20 @@
     period = 8 * frames
     circle = 2.0 * np.pi / period * np.arange(period)
     product = odd[:, None] * odd[None, :] % period
-    highs, lows = [], []
-    for wave in (np.cos(circle), np.sin(circle)):
-        wave = wave.astype(np.float32)
-        high = wave.astype(BF16)
-        low = (wave - high.astype(np.float32)).astype(BF16)
-        highs.append(high[product])
-        lows.append(low[product])
+    waves = np.stack([wave.astype(BF16)[product] for wave in (np.cos(circle), np.sin(circle))])
     half = np.pi * odd / (4.0 * frames)
     turn = np.stack([np.cos(half), np.sin(half)]) / frames
-    return np.stack(highs), np.stack(lows), turn.astype(np.float32)
-
-
-def halves(value):
-    high = value.astype(BF16)
-    return high, (value - high.astype(F32)).astype(BF16)
-
-
-def product(parts, table_high, table_low):
-    high, low = parts
-    total = jnp.dot(high, table_high, preferred_element_type=F32)
-    if table_low is not None:
-        total += jnp.dot(high, table_low, preferred_element_type=F32)
-    if low is not None:
-        total += jnp.dot(low, table_high, preferred_element_type=F32)
-    return total
+    return waves, turn.astype(np.float32)
 
 
 def kernel(
     sizes,
     values_hbm, first_hbm, second_hbm, early_hbm, late_hbm, early_skip_hbm, late_skip_hbm,
-    targets_hbm, rows_hbm, ids_hbm, high_hbm, low_hbm, turn_hbm,
+    targets_hbm, rows_hbm, ids_hbm, waves_hbm, turn_hbm,
     values_out, first_out, second_out, early_out, late_out,
     values_ref, first_ref, second_ref, early_ref, late_ref, early_skip_ref, late_skip_ref,
-    targets_ref, rows_ref, ids_ref, high_ref, low_ref, turn_ref,
-    pool, out_send, out_recv, back_send, back_recv, pair_send, pair_recv, ring_send, ring_recv,
+    rows_ref, ids_ref, waves_ref, turn_ref,
+    pool, units_ref, out_send, out_recv, back_send, back_recv, pair_send, pair_recv, ring_send, ring_recv,
     mixed_one, mixed_two, early_spec, late_spec, signal_spec, hidden_spec, counts_ref,
     load_sem, pool_send_sem, pool_recv_sem, pass_send_sem, pass_recv_sem,
     out_send_sem, out_recv_sem, back_send_sem, back_recv_sem,
@@ -307,10 +287,8 @@
     loads = {
         name: pltpu.make_async_copy(source, target, load_sem.at[i])
         for i, (name, source, target) in enumerate((
-            ("targets", targets_hbm.at[0], targets_ref),
             ("early", early_hbm, early_ref),
-            ("high", high_hbm, high_ref),
-            ("low", low_hbm, low_ref),
+            ("waves", waves_hbm, waves_ref),
             ("late", late_hbm, late_ref),
             ("turn", turn_hbm, turn_ref),
             ("values", values_hbm.at[0], values_ref),
@@ -320,6 +298,7 @@
             ("late_skip", late_skip_hbm, late_skip_ref),
             ("rows", rows_hbm.at[0], rows_ref),
             ("ids", ids_hbm, ids_ref),
+            ("targets", targets_hbm.at[0], pool.at[me]),
         ))
     }
     for load in loads.values():
@@ -331,10 +310,6 @@
             device_id=device, device_id_type=MESH,
         )
 
-    loads["targets"].wait()
-    full = targets_ref[...].astype(F32)
-    norm = jnp.sqrt(jnp.sum(full * full, axis=-1, keepdims=True) + EPSILON)
-    pool[me] = (full / norm).astype(BF16)
     pl.semaphore_wait(barrier, len(peers))
 
     def piece(owner, h):
@@ -346,8 +321,9 @@
             (y_chip, 0, x_chip), (x_chip, 1, y_chip),
         )[n]
         block = piece(owner, h)
-        return remote(
-            block, block, pool_send_sem.at[n], pool_recv_sem.at[n], (to * 2 + core, here)
+        source = targets_hbm.at[0, pl.ds(h * part, part)] if n < 4 else block
+        return remote(
+            source, block, pool_send_sem.at[n], pool_recv_sem.at[n], (to * 2 + core, here)
         )
 
     def pool_arrival(n):
@@ -363,6 +339,9 @@
     def passed(n, lane):
         if n == 6:
             block = pool.at[chip * 2 + lane]
+            return remote(
+                targets_hbm.at[0], block, pass_send_sem.at[n], pass_recv_sem.at[n], (partner, here)
+            )
         else:
             owner, h = (
                 (x_chip, 1), (y_chip, 0), (x_chip, 0), (y_chip, 1), (d_chip, 0), (d_chip, 1)
@@ -380,15 +359,19 @@
         pool_copy(n).start()
     pass_copy(6).start()
 
-    def forward(parts):
-        return tuple(product(parts, high_ref[i], low_ref[i]) for i in (0, 1))
-
-    def inverse(cosine, sine, fine=True):
-        total = None
-        for i, wave in enumerate((cosine, sine)):
-            part = product((wave.astype(BF16), None), high_ref[i], low_ref[i] if fine else None)
-            total = part if total is None else total + part
-        return total
+    def normalize(slot):
+        full = pool[slot].astype(F32)
+        norm = jnp.sqrt(jnp.sum(full * full, axis=-1, keepdims=True) + EPSILON)
+        units_ref[slot] = (full * (1.0 / norm)).astype(BF16)
+
+    def forward(signal):
+        signal = signal.astype(BF16)
+        return tuple(jnp.dot(signal, waves_ref[i], preferred_element_type=F32) for i in (0, 1))
+
+    def inverse(cosine, sine):
+        return jnp.dot(
+            cosine.astype(BF16), waves_ref[0], preferred_element_type=F32
+        ) + jnp.dot(sine.astype(BF16), waves_ref[1], preferred_element_type=F32)
 
     def unshifted(spec):
         cosine, sine = spec
@@ -407,28 +390,34 @@
         cosine, sine = spec
         return inverse(cosine * ref[0] - sine * ref[1], cosine * ref[1] + sine * ref[0])
 
-    def correlated(spec, ref, fine=True):
+    def correlated(spec, refs, lines):
         cosine, sine = spec
-        return inverse(cosine * ref[0] + sine * ref[1], sine * ref[0] - cosine * ref[1], fine)
+        waves = []
+        for ref in refs:
+            real, imaginary = ref[0, lines], ref[1, lines]
+            waves.append((cosine * real + sine * imaginary, sine * real - cosine * imaginary))
+        joined = inverse(*(jnp.concatenate(wave, axis=0) for wave in zip(*waves)))
+        count = joined.shape[0] // len(refs)
+        return [joined[i * count : (i + 1) * count] for i in range(len(refs))]
 
     def column(row):
         return jnp.broadcast_to(row, (8, channels)).T[:, 0:1]
 
-    for name in ("early", "high", "low", "turn"):
+    for name in ("early", "waves", "turn"):
         loads[name].wait()
-    keep(early_spec, unshifted(forward(halves(early_ref[...]))))
+    keep(early_spec, unshifted(forward(early_ref[...])))
     loads["late"].wait()
-    keep(late_spec, unshifted(forward(halves(late_ref[...]))))
+    keep(late_spec, unshifted(forward(late_ref[...])))
     for name in ("values", "early_skip", "late_skip"):
         loads[name].wait()
     early_skip = column(early_skip_ref[...])
     late_skip = column(late_skip_ref[...])
-    spec = forward((values_ref[...], None))
+    spec = forward(values_ref[...])
     mixed_one[...] = convolved(spec, early_spec) + early_skip * values_ref[...].astype(F32)
     signal_waves = spec
     loads["first"].wait()
     hidden = first_ref[...].astype(F32) * mixed_one[...]
-    spec = forward((hidden.astype(BF16), None))
+    spec = forward(hidden)
     mixed_two[...] = convolved(spec, late_spec) + late_skip * hidden
 
     loads["second"].wait()
@@ -436,18 +425,41 @@
     for s in range(stages):
         out_send[s] = output[:, s * segment : (s + 1) * segment].astype(BF16)
 
-    def exchange(k, send, recv, send_sem, recv_sem):
-        peer = lax.rem(here + k, stages)
-        return remote(send.at[peer], recv.at[here], send_sem.at[k], recv_sem.at[k], (me, peer))
-
-    def exchange_arrival(k, send, recv, send_sem, recv_sem):
-        peer = lax.rem(here + stages - k, stages)
-        return remote(send.at[peer], recv.at[peer], send_sem.at[k], recv_sem.at[k], (me, peer))
-
-    out_group = (out_send, out_recv, out_send_sem, out_recv_sem)
-    back_group = (back_send, back_recv, back_send_sem, back_recv_sem)
-    for k in range(1, stages):
-        exchange(k, *out_group).start()
+    low_side = 1 - (2 * here) // stages
+
+    def far_peer(j):
+        high = stages - 1 - j
+        up = high - (here - high + stages) // stages
+        down = j + (j - here + stages) // stages
+        return low_side * up + (1 - low_side) * down
+
+    def out_copy(peer):
+        return remote(
+            out_send.at[peer], out_recv.at[here], out_send_sem.at[peer], out_recv_sem.at[here],
+            (me, peer),
+        )
+
+    def out_arrival(peer):
+        return remote(
+            out_send.at[peer], out_recv.at[peer], out_send_sem.at[peer], out_recv_sem.at[peer],
+            (me, peer),
+        )
+
+    def back_copy(j, peer):
+        return remote(
+            back_send.at[j, peer], back_recv.at[j, here],
+            back_send_sem.at[j, peer], back_recv_sem.at[j, here], (me, peer),
+        )
+
+    def back_arrival(j, peer):
+        return remote(
+            back_send.at[j, peer], back_recv.at[j, peer],
+            back_send_sem.at[j, peer], back_recv_sem.at[j, peer], (me, peer),
+        )
+
+    others = [lax.rem(here + k, stages) for k in range(1, stages)]
+    for j in range(stages - 1):
+        out_copy(far_peer(j)).start()
     out_recv[here] = out_send[here]
 
     pool_arrival(1).wait_recv()
@@ -475,164 +487,211 @@
     for c in range(chips):
         counts_ref[c] = counts[c * 2 * segment : (c + 1) * 2 * segment, :]
 
-    self_units = pool[me].astype(F32).T
-
+    loads["targets"].wait()
+    normalize(me)
+    self_units = units_ref[me].astype(F32).T
+    pass_arrival(6).wait_recv()
+    normalize(partner)
     for n in (2, 3):
         pool_arrival(n).wait_recv()
         pass_copy(n).start()
-
-    for k in range(1, stages):
-        exchange_arrival(k, *out_group).wait_recv()
+    for c in (x_chip, y_chip):
+        normalize(c * 2 + core)
+    for n in (1, 0, 2, 3):
+        pass_arrival(n).wait_recv()
+    for c in (x_chip, y_chip):
+        normalize(c * 2 + 1 - core)
+    for n in (4, 5):
+        pool_arrival(n).wait_recv()
+        pass_copy(n).start()
+    normalize(d_chip * 2 + core)
+
+    for peer in others:
+        out_arrival(peer).wait_recv()
     rows = jnp.concatenate([out_recv[s] for s in range(stages)], axis=0).astype(F32)
     radius = jnp.sqrt(jnp.sum(rows * rows, axis=0, keepdims=True) + EPSILON)
-    unit_rows = rows / radius
+    unit_rows = rows * (1.0 / radius)
     anchors = unit_rows.astype(BF16)
     positive = jnp.exp(jnp.sum(anchors.astype(F32) * self_units, axis=0, keepdims=True) * INVERSE_TEMP)
+    alignment = jnp.sum(unit_rows * self_units, axis=0, keepdims=True)
 
     upper = lax.broadcasted_iota(jnp.int32, (2 * segment, 1), 0) < segment
 
     def against(c):
-        units = pool[pl.ds(c * 2, 2)].reshape(2 * segment, depth)
+        units = units_ref[pl.ds(c * 2, 2)].reshape(2 * segment, depth)
         own_id = ids_ref[me]
         allowed = [jnp.where(ids_ref[c * 2 + i] != own_id, 1.0, 0.0).astype(F32) for i in (0, 1)]
-        scores = jnp.dot(units, anchors, preferred_element_type=F32) * INVERSE_TEMP
-        weights = counts_ref[c] * jnp.where(upper, allowed[0], allowed[1]) * jnp.exp(scores)
+        cosines = jnp.dot(units, anchors, preferred_element_type=F32)
+        weights = (
+            counts_ref[c] * jnp.where(upper, allowed[0], allowed[1]) * jnp.exp(cosines * INVERSE_TEMP)
+        )
+        rounded = weights.astype(BF16)
         return (
             jnp.sum(weights, axis=0, keepdims=True),
+            jnp.sum(rounded.astype(F32) * cosines, axis=0, keepdims=True),
             jnp.dot(weights.T.astype(BF16), units, preferred_element_type=F32),
         )
 
-    pass_arrival(6).wait_recv()
-    summed, numerator = against(chip)
+    summed, turned, numerator = against(chip)
     totals = positive + summed
-    for c, pieces in ((x_chip, (0, 2)), (y_chip, (1, 3)), (d_chip, (4, 5))):
-        if pieces == (4, 5):
-            for n in pieces:
-                pool_arrival(n).wait_recv()
-                pass_copy(n).start()
-        for n in pieces:
-            pass_arrival(n).wait_recv()
-        summed, partial = against(c)
+    for c in (x_chip, y_chip, d_chip):
+        if c is d_chip:
+            for n in (4, 5):
+                pass_arrival(n).wait_recv()
+            normalize(c * 2 + 1 - core)
+        summed, partial_turned, partial = against(c)
         totals += summed
+        turned += partial_turned
         numerator += partial
-    anchor_grad = ((positive / totals - 1.0) * self_units + numerator.T / totals) * (
-        INVERSE_TEMP * LOSS_SCALE
-    )
-    frame_grad = (
-        anchor_grad - unit_rows * jnp.sum(unit_rows * anchor_grad, axis=0, keepdims=True)
-    ) / radius
-    for s in range(stages):
-        back_send[s] = frame_grad[s * channels : (s + 1) * channels, :].astype(BF16)
-    for k in range(1, stages):
-        exchange(k, *back_group).start()
-    back_recv[here] = back_send[here]
-    for k in range(1, stages):
-        exchange_arrival(k, *back_group).wait_recv()
-
-    half = channels // 2
+    scale = INVERSE_TEMP * LOSS_SCALE / radius
+    pull = (positive / totals - 1.0) * scale
+    push = scale / totals
+    tilt = pull * alignment + push * turned
+    chunks, _, size, _ = back_recv.shape
+    for j in range(chunks):
+        for s in range(stages):
+            at = slice(s * channels + j * size, s * channels + (j + 1) * size)
+            back_send[j, s] = (
+                pull * self_units[at] + push * numerator[:, at].T - tilt * unit_rows[at]
+            ).astype(BF16)
+        for i in range(stages - 1):
+            back_copy(j, far_peer(i)).start()
+        back_recv[j, here] = back_send[j, here]
+
+    half = size // 2
     shard = half // chips
 
-    def pair_copy(which, lane):
-        return remote(
-            pair_send.at[which, lane], pair_recv.at[which],
-            pair_send_sem.at[which], pair_recv_sem.at[which], (partner, here),
-        )
-
-    def spread(which, update):
+    def pair_copy(which, j, lane):
+        return remote(
+            pair_send.at[which, j, lane], pair_recv.at[which, j],
+            pair_send_sem.at[which, j], pair_recv_sem.at[which, j], (partner, here),
+        )
+
+    def spread(which, j, update):
         for i in (0, 1):
-            pair_send[which, i] = update[i * half : (i + 1) * half, :].astype(BF16)
-        pair_copy(which, 1 - core).start()
-
-    def ring_copy(which, n):
-        return remote(
-            ring_send.at[which, near[n]], ring_recv.at[which, n],
-            ring_send_sem.at[which, n], ring_recv_sem.at[which, n], (near[n] * 2 + core, here),
-        )
-
-    def gather(which):
-        pair_copy(which, core).wait_recv()
-        joined = pair_send[which, core].astype(F32) + pair_recv[which].astype(F32)
-        for j in range(chips):
-            ring_send[which, j] = joined[j * shard : (j + 1) * shard, :].astype(BF16)
+            pair_send[which, j, i] = update[i * half : (i + 1) * half, :].astype(BF16)
+        pair_copy(which, j, 1 - core).start()
+
+    def ring_copy(which, j, n):
+        return remote(
+            ring_send.at[which, j, near[n]], ring_recv.at[which, j, n],
+            ring_send_sem.at[which, j, n], ring_recv_sem.at[which, j, n],
+            (near[n] * 2 + core, here),
+        )
+
+    def gather(which, j):
+        pair_copy(which, j, core).wait_recv()
+        joined = pair_send[which, j, core].astype(F32) + pair_recv[which, j].astype(F32)
+        for c in range(chips):
+            ring_send[which, j, c] = joined[c * shard : (c + 1) * shard, :].astype(BF16)
         for n in (2, 0, 1):
-            ring_copy(which, n).start()
-
-    def share_copy(which, target, n):
-        block = target.at[core * chips + chip]
-        return remote(
-            block, block, share_send_sem.at[which, n], share_recv_sem.at[which, n],
+            ring_copy(which, j, n).start()
+
+    targets_out = (early_out, late_out)
+
+    def share_copy(which, j, n):
+        block = targets_out[which].at[j, core, chip]
+        return remote(
+            block, block, share_send_sem.at[which, j, n], share_recv_sem.at[which, j, n],
             (near[n] * 2 + core, here),
         )
 
-    def share_arrival(which, target, n):
-        block = target.at[core * chips + near[n]]
-        return remote(
-            block, block, share_send_sem.at[which, n], share_recv_sem.at[which, n],
+    def share_arrival(which, j, n):
+        block = targets_out[which].at[j, core, near[n]]
+        return remote(
+            block, block, share_send_sem.at[which, j, n], share_recv_sem.at[which, j, n],
             (near[n] * 2 + core, here),
         )
 
     sources = near + (chip,)
 
-    def last_copy(which, target, n):
-        block = target.at[core * chips + sources[n]]
-        return remote(
-            block, block, last_send_sem.at[which, n], last_recv_sem.at[which, n], (partner, here)
-        )
-
-    def last_arrival(which, target, n):
-        block = target.at[(1 - core) * chips + sources[n]]
-        return remote(
-            block, block, last_send_sem.at[which, n], last_recv_sem.at[which, n], (partner, here)
-        )
-
-    def share(which, target):
-        total = ring_send[which, chip].astype(F32)
+    def last_copy(which, j, n):
+        block = targets_out[which].at[j, core, sources[n]]
+        return remote(
+            block, block, last_send_sem.at[which, j, n], last_recv_sem.at[which, j, n],
+            (partner, here),
+        )
+
+    def last_arrival(which, j, n):
+        block = targets_out[which].at[j, 1 - core, sources[n]]
+        return remote(
+            block, block, last_send_sem.at[which, j, n], last_recv_sem.at[which, j, n],
+            (partner, here),
+        )
+
+    def share(which, j):
+        total = ring_send[which, j, chip].astype(F32)
         for n in range(3):
-            ring_copy(which, n).wait_recv()
-            total += ring_recv[which, n].astype(F32)
-        target[core * chips + chip] = total.astype(BF16)
+            ring_copy(which, j, n).wait_recv()
+            total += ring_recv[which, j, n].astype(F32)
+        targets_out[which][j, core, chip] = total.astype(BF16)
         for n in (2, 0, 1):
-            share_copy(which, target, n).start()
-        last_copy(which, target, 3).start()
-
-    def relay(which, target):
+            share_copy(which, j, n).start()
+        last_copy(which, j, 3).start()
+
+    def relay(which, j):
         for n in range(3):
-            share_arrival(which, target, n).wait_recv()
-            last_copy(which, target, n).start()
-
-    cotangent = jnp.concatenate([back_recv[s] for s in range(stages)], axis=1).astype(F32)
-    late_drive = cotangent * second_ref[...].astype(F32)
-    spec = forward((late_drive.astype(BF16), None))
-    hidden_grad = correlated(spec, late_spec) + late_skip * late_drive
-    spread(1, correlated(spec, hidden_spec, fine=False))
-    early_drive = hidden_grad * first_ref[...].astype(F32)
-    spec = forward((early_drive.astype(BF16), None))
-    spread(0, correlated(spec, signal_spec, fine=False))
-    gather(1)
-    second_out[0] = (cotangent * mixed_two[...]).astype(BF16)
-    first_out[0] = (hidden_grad * mixed_one[...]).astype(BF16)
-    gather(0)
-    values_out[0] = (correlated(spec, early_spec) + early_skip * early_drive).astype(BF16)
-    share(1, late_out)
-    share(0, early_out)
-    relay(1, late_out)
-    relay(0, early_out)
+            share_arrival(which, j, n).wait_recv()
+            last_copy(which, j, n).start()
+
+    def backward(j):
+        for peer in others:
+            back_arrival(j, peer).wait_recv()
+        lines = slice(j * size, (j + 1) * size)
+        cotangent = jnp.concatenate([back_recv[j, s] for s in range(stages)], axis=1).astype(F32)
+        late_drive = cotangent * second_ref[lines].astype(F32)
+        update, adjoint = correlated(forward(late_drive), (hidden_spec, late_spec), lines)
+        spread(1, j, update)
+        hidden_grad = adjoint + late_skip[lines] * late_drive
+        early_drive = hidden_grad * first_ref[lines].astype(F32)
+        update, adjoint = correlated(forward(early_drive), (signal_spec, early_spec), lines)
+        spread(0, j, update)
+        values_out[0, lines] = (adjoint + early_skip[lines] * early_drive).astype(BF16)
+        second_out[0, lines] = (cotangent * mixed_two[lines]).astype(BF16)
+        first_out[0, lines] = (hidden_grad * mixed_one[lines]).astype(BF16)
+
+    for j in range(chunks):
+        backward(j)
+        if j:
+
+            @pl.when(core == 1)
+            def _():
+                gather(1, j - 1)
+                gather(0, j - 1)
+
+        if j + 1 < chunks:
+
+            @pl.when(core == 0)
+            def _():
+                gather(1, j)
+                gather(0, j)
+
+    for which in (1, 0):
+        gather(which, chunks - 1)
+    for j in range(chunks):
+        for which in (1, 0):
+            share(which, j)
+    for j in range(chunks):
+        for which in (1, 0):
+            relay(which, j)
 
     for n in range(6):
         pool_copy(n).wait_send()
     for n in range(7):
         pass_copy(n).wait_send()
-    for k in range(1, stages):
-        exchange(k, *out_group).wait_send()
-        exchange(k, *back_group).wait_send()
-    for which, target in ((1, late_out), (0, early_out)):
-        pair_copy(which, 1 - core).wait_send()
-        for n in range(3):
-            ring_copy(which, n).wait_send()
-            share_copy(which, target, n).wait_send()
-        for n in range(4):
-            last_copy(which, target, n).wait_send()
-            last_arrival(which, target, n).wait_recv()
+    for peer in others:
+        out_copy(peer).wait_send()
+        for j in range(chunks):
+            back_copy(j, peer).wait_send()
+    for j in range(chunks):
+        for which in (1, 0):
+            pair_copy(which, j, 1 - core).wait_send()
+            for n in range(3):
+                ring_copy(which, j, n).wait_send()
+                share_copy(which, j, n).wait_send()
+            for n in range(4):
+                last_copy(which, j, n).wait_send()
+                last_arrival(which, j, n).wait_recv()
 
 
 def finish(
@@ -668,41 +727,48 @@
             values, gates_first, gates_second, filter_early, filter_late, skip_early, skip_late,
             targets, negative_rows, recording_ids,
         )
-    high, low, turn = tables(frames)
+    waves, turn = tables(frames)
     chips = records // 2
-    half = channels // 2
+    size = channels // CHUNKS
+    half = size // 2
     shard = half // chips
     blocks, draws = negative_rows.shape[1:]
     vmem = pl.BlockSpec(memory_space=pltpu.VMEM)
     hbm = pl.BlockSpec(memory_space=pltpu.HBM)
     stream = pltpu.VMEM(values.shape, BF16)
-    update = pltpu.VMEM((records, shard, frames), BF16)
+    gradient = (CHUNKS, 2, chips, shard, frames)
+    update = pltpu.VMEM(gradient, BF16)
     exchange = pltpu.VMEM((stages, channels, segment), BF16)
     plane = pltpu.VMEM((channels, frames), F32)
     narrow = pltpu.VMEM((channels, frames), BF16)
     spec = pltpu.VMEM((2, channels, frames), F32)
     skip = pltpu.VMEM((1, channels), F32)
-    table = pltpu.VMEM(high.shape, BF16)
+    back = pltpu.VMEM((CHUNKS, stages, size, segment), BF16)
     semaphores = pltpu.SemaphoreType.DMA
     results = pl.pallas_call(
         functools.partial(kernel, (records, stages)),
         out_shape=(stream, stream, stream, update, update),
-        in_specs=[hbm] * 13,
+        in_specs=[hbm] * 12,
         out_specs=(vmem,) * 5,
         scratch_shapes=[
             narrow, narrow, narrow, plane, plane, skip, skip,
-            pltpu.VMEM((segment, depth), BF16), pltpu.VMEM((blocks, draws), jnp.int32),
-            pltpu.SMEM((records,), jnp.int32), table, table, pltpu.VMEM(turn.shape, F32),
-            pltpu.VMEM((records, segment, depth), BF16),
-            exchange, exchange, exchange, exchange,
-            pltpu.VMEM((2, 2, half, frames), BF16), pltpu.VMEM((2, half, frames), BF16),
-            pltpu.VMEM((2, chips, shard, frames), BF16), pltpu.VMEM((2, 3, shard, frames), BF16),
+            pltpu.VMEM((blocks, draws), jnp.int32),
+            pltpu.SMEM((records,), jnp.int32), pltpu.VMEM(waves.shape, BF16),
+            pltpu.VMEM(turn.shape, F32),
+            pltpu.VMEM((records, segment, depth), BF16), pltpu.VMEM((records, segment, depth), BF16),
+            exchange, exchange, back, back,
+            pltpu.VMEM((2, CHUNKS, 2, half, frames), BF16), pltpu.VMEM((2, CHUNKS, half, frames), BF16),
+            pltpu.VMEM((2, CHUNKS, chips, shard, frames), BF16),
+            pltpu.VMEM((2, CHUNKS, 3, shard, frames), BF16),
             plane, plane, spec, spec, spec, spec,
             pltpu.VMEM((chips, 2 * segment, segment), F32),
-            semaphores((13,)), semaphores((6,)), semaphores((6,)), semaphores((7,)), semaphores((7,)),
-            semaphores((stages,)), semaphores((stages,)), semaphores((stages,)), semaphores((stages,)),
-            semaphores((2,)), semaphores((2,)), semaphores((2, 3)), semaphores((2, 3)),
-            semaphores((2, 3)), semaphores((2, 3)), semaphores((2, 4)), semaphores((2, 4)),
+            semaphores((12,)), semaphores((6,)), semaphores((6,)), semaphores((7,)), semaphores((7,)),
+            semaphores((stages,)), semaphores((stages,)),
+            semaphores((CHUNKS, stages)), semaphores((CHUNKS, stages)),
+            semaphores((2, CHUNKS)), semaphores((2, CHUNKS)),
+            semaphores((2, CHUNKS, 3)), semaphores((2, CHUNKS, 3)),
+            semaphores((2, CHUNKS, 3)), semaphores((2, CHUNKS, 3)),
+            semaphores((2, CHUNKS, 4)), semaphores((2, CHUNKS, 4)),
         ],
         compiler_params=pltpu.CompilerParams(
             collective_id=0, has_side_effects=True, vmem_limit_bytes=VMEM_BYTES
@@ -712,10 +778,10 @@
         for operand in (
             values, gates_first, gates_second, filter_early, filter_late,
             skip_early[None], skip_late[None], targets, negative_rows, recording_ids,
-            jnp.asarray(high), jnp.asarray(low), jnp.asarray(turn),
+            jnp.asarray(waves), jnp.asarray(turn),
         )
     ))
-    wide = (records, shard, frames)
+    wide = gradient
     *streams, early, late = pl.pallas_call(
         functools.partial(finish, frames),
         out_shape=(jax.ShapeDtypeStruct(values.shape, BF16),) * 3 + (jax.ShapeDtypeStruct(wide, F32),) * 2,

time: 42.4 us -> 38 us (0.90)
  Pallas kernels: 41.6 us -> 37.2 us
    pallas_call x1, Pallas kernels: 40.3 us -> 35.9 us  [local(): pl.pallas_call(functools.partial(kernel, (records, stages)), out_shape=(s...]
where the time goes in v2:
time: 38 us; the launch traced here: 37.8 us
  Pallas kernels  37.2 us (98%)
  between operations  0.64 us (2%)
    pallas_call x1, Pallas kernels, local(): pl.pallas_call(functools.partial(kernel, (records, stages)), out_shape=(s...  35.9 us
    pallas_call x1, Pallas kernels, local(): pl.pallas_call(functools.partial(finish, frames), out_shape=(jax.ShapeDty...  1.27 us

profile of v2, /device:TPU:0, one launch (start us, length us, event | category | flops | bytes accessed | tf_op | source)
XLA Modules:
  0.0 37.8 jit_solution(1612176901431523812)
XLA Ops:
  0.6 35.9 %shard_map.155 = (bf16[1,256,512]{2,1,0:T(8,128)(2,1)S(1)}, bf16[1,256,512]{2,1,0:T(8,128)(2,1)S(1)}, bf16[1,256,512]{2,1,0:T(8,128)(2,1)S(1)}, bf16[2,2,4,16,51...) custom-call(bf16[1,256,512]{2,1,0:T(8,128)(2,1)} %values_hbm.1, bf16[1,256,512]{2,1,0:T(8,128)(2,1)} %first_hbm.1, ...), custom_call_target="tpu_custom_call" | custom-call | tf_op jit(solution)/shard_map/pallas_call | solution.py:748
  36.6 1.3 %shard_map.156 = (bf16[1,256,512]{2,1,0:T(8,128)(2,1)}, bf16[1,256,512]{2,1,0:T(8,128)(2,1)}, bf16[1,256,512]{2,1,0:T(8,128)(2,1)}, f32[2,2,4,16,512]{4,3,2,1,0:T(8,128)}, f32[2,2,4,16,512]{4,3,2,1,0:T(8,128)}) custom-call(bf16[1,256,512]{2,1,0:T(8,128)(2,1)S(1)} %get-tuple-element.15.values_in, bf16[1,256,512]{2,1,0:T(8,128)(2,1)S(1)} %get-tuple-element.16.first_in, ...), custom_call_target="tpu_custom_call" | custom-call | tf_op jit(solution)/shard_map/pallas_call | solution.py:785

commit v3 on v2

--- a/solution.py
+++ b/solution.py
@@ -253,14 +253,11 @@
     values_hbm, first_hbm, second_hbm, early_hbm, late_hbm, early_skip_hbm, late_skip_hbm,
     targets_hbm, rows_hbm, ids_hbm, waves_hbm, turn_hbm,
     values_out, first_out, second_out, early_out, late_out,
-    values_ref, first_ref, second_ref, early_ref, late_ref, early_skip_ref, late_skip_ref,
-    rows_ref, ids_ref, waves_ref, turn_ref,
-    pool, units_ref, out_send, out_recv, back_send, back_recv, pair_send, pair_recv, ring_send, ring_recv,
-    mixed_one, mixed_two, early_spec, late_spec, signal_spec, hidden_spec, counts_ref,
-    load_sem, pool_send_sem, pool_recv_sem, pass_send_sem, pass_recv_sem,
-    out_send_sem, out_recv_sem, back_send_sem, back_recv_sem,
-    pair_send_sem, pair_recv_sem, ring_send_sem, ring_recv_sem,
-    share_send_sem, share_recv_sem, last_send_sem, last_recv_sem,
+    streams_ref, filters_ref, skips_ref, rows_ref, ids_ref, waves_ref, turn_ref,
+    pool, out_send, out_recv, back_send, back_recv, pair_send, pair_recv, ring_send, ring_recv,
+    mixed_one, mixed_two, early_spec, late_spec, signal_spec, hidden_spec, drawn_ref,
+    load_sem, send_sem, pool_recv_sem, pass_recv_sem, out_recv_sem, back_recv_sem,
+    pair_recv_sem, ring_recv_sem, share_recv_sem, last_recv_sem,
 ):
     records, stages = sizes
     chips = records // 2
@@ -279,30 +276,33 @@
     part = segment // 2
 
     barrier = pltpu.get_barrier_semaphore()
-    peers = [(partner, here)] + [(c * 2 + core, here) for c in near]
-    peers += [(me, lax.rem(here + k, stages)) for k in range(1, stages)]
+    peers = [(me, lax.rem(here + k, stages)) for k in range(1, stages)]
+    peers += [(c * 2 + core, here) for c in near] + [(partner, here)]
     for peer in peers:
         pl.semaphore_signal(barrier, inc=1, device_id=peer, device_id_type=MESH)
 
-    loads = {
-        name: pltpu.make_async_copy(source, target, load_sem.at[i])
-        for i, (name, source, target) in enumerate((
-            ("early", early_hbm, early_ref),
-            ("waves", waves_hbm, waves_ref),
-            ("late", late_hbm, late_ref),
-            ("turn", turn_hbm, turn_ref),
-            ("values", values_hbm.at[0], values_ref),
-            ("first", first_hbm.at[0], first_ref),
-            ("second", second_hbm.at[0], second_ref),
-            ("early_skip", early_skip_hbm, early_skip_ref),
-            ("late_skip", late_skip_hbm, late_skip_ref),
-            ("rows", rows_hbm.at[0], rows_ref),
-            ("ids", ids_hbm, ids_ref),
-            ("targets", targets_hbm.at[0], pool.at[me]),
-        ))
-    }
-    for load in loads.values():
+    loads = [
+        pltpu.make_async_copy(source, target, load_sem.at[i])
+        for i, source, target in (
+            (0, early_hbm, filters_ref.at[0]),
+            (1, waves_hbm, waves_ref),
+            (0, late_hbm, filters_ref.at[1]),
+            (2, turn_hbm, turn_ref),
+            (3, values_hbm.at[0], streams_ref.at[0]),
+            (3, first_hbm.at[0], streams_ref.at[1]),
+            (3, second_hbm.at[0], streams_ref.at[2]),
+            (4, early_skip_hbm, skips_ref.at[0]),
+            (4, late_skip_hbm, skips_ref.at[1]),
+            (5, rows_hbm.at[0], rows_ref),
+            (6, ids_hbm, ids_ref),
+            (7, targets_hbm.at[0], pool.at[me]),
+        )
+    ]
+    for load in loads:
         load.start()
+
+    def loaded(i, ref):
+        pltpu.make_async_copy(ref, ref, load_sem.at[i]).wait()
 
     def remote(source, target, send, recv, device):
         return pltpu.make_async_remote_copy(
@@ -311,6 +311,12 @@
         )
 
     pl.semaphore_wait(barrier, len(peers))
+
+    def sent(ref, sem):
+        remote(ref, ref, sem, sem, (partner, here)).wait_send()
+
+    def landed(ref, sem):
+        remote(ref, ref, sem, sem, (partner, here)).wait_recv()
 
     def piece(owner, h):
         return pool.at[owner * 2 + core, pl.ds(h * part, part)]
@@ -323,7 +329,7 @@
         block = piece(owner, h)
         source = targets_hbm.at[0, pl.ds(h * part, part)] if n < 4 else block
         return remote(
-            source, block, pool_send_sem.at[n], pool_recv_sem.at[n], (to * 2 + core, here)
+            source, block, send_sem.at[0], pool_recv_sem.at[n], (to * 2 + core, here)
         )
 
     def pool_arrival(n):
@@ -333,36 +339,31 @@
         )[n]
         block = piece(owner, h)
         return remote(
-            block, block, pool_send_sem.at[n], pool_recv_sem.at[n], (to * 2 + core, here)
-        )
-
-    def passed(n, lane):
+            block, block, send_sem.at[0], pool_recv_sem.at[n], (to * 2 + core, here)
+        )
+
+    def pass_copy(n):
         if n == 6:
-            block = pool.at[chip * 2 + lane]
+            block = pool.at[me]
             return remote(
-                targets_hbm.at[0], block, pass_send_sem.at[n], pass_recv_sem.at[n], (partner, here)
+                targets_hbm.at[0], block, send_sem.at[1], pass_recv_sem.at[0], (partner, here)
             )
         else:
             owner, h = (
                 (x_chip, 1), (y_chip, 0), (x_chip, 0), (y_chip, 1), (d_chip, 0), (d_chip, 1)
             )[n]
-            block = pool.at[owner * 2 + lane, pl.ds(h * part, part)]
-        return remote(block, block, pass_send_sem.at[n], pass_recv_sem.at[n], (partner, here))
-
-    def pass_copy(n):
-        return passed(n, core)
-
-    def pass_arrival(n):
-        return passed(n, 1 - core)
+            block = piece(owner, h)
+        return remote(
+            block, block, send_sem.at[1], pass_recv_sem.at[1 + n // 4], (partner, here)
+        )
 
     for n in range(4):
         pool_copy(n).start()
     pass_copy(6).start()
 
-    def normalize(slot):
-        full = pool[slot].astype(F32)
-        norm = jnp.sqrt(jnp.sum(full * full, axis=-1, keepdims=True) + EPSILON)
-        units_ref[slot] = (full * (1.0 / norm)).astype(BF16)
+    def normalized(rows):
+        norm = jnp.sqrt(jnp.sum(rows * rows, axis=-1, keepdims=True) + EPSILON)
+        return (rows * (1.0 / norm)).astype(BF16)
 
     def forward(signal):
         signal = signal.astype(BF16)
@@ -403,24 +404,23 @@
     def column(row):
         return jnp.broadcast_to(row, (8, channels)).T[:, 0:1]
 
-    for name in ("early", "waves", "turn"):
-        loads[name].wait()
-    keep(early_spec, unshifted(forward(early_ref[...])))
-    loads["late"].wait()
-    keep(late_spec, unshifted(forward(late_ref[...])))
-    for name in ("values", "early_skip", "late_skip"):
-        loads[name].wait()
-    early_skip = column(early_skip_ref[...])
-    late_skip = column(late_skip_ref[...])
+    loaded(0, filters_ref)
+    loaded(1, waves_ref)
+    loaded(2, turn_ref)
+    keep(early_spec, unshifted(forward(filters_ref[0])))
+    keep(late_spec, unshifted(forward(filters_ref[1])))
+    loaded(3, streams_ref)
+    loaded(4, skips_ref)
+    values_ref, first_ref, second_ref = (streams_ref.at[i] for i in range(3))
+    early_skip = column(skips_ref[0])
+    late_skip = column(skips_ref[1])
     spec = forward(values_ref[...])
     mixed_one[...] = convolved(spec, early_spec) + early_skip * values_ref[...].astype(F32)
     signal_waves = spec
-    loads["first"].wait()
     hidden = first_ref[...].astype(F32) * mixed_one[...]
     spec = forward(hidden)
     mixed_two[...] = convolved(spec, late_spec) + late_skip * hidden
 
-    loads["second"].wait()
     output = second_ref[...].astype(F32) * mixed_two[...]
     for s in range(stages):
         out_send[s] = output[:, s * segment : (s + 1) * segment].astype(BF16)
@@ -435,29 +435,15 @@
 
     def out_copy(peer):
         return remote(
-            out_send.at[peer], out_recv.at[here], out_send_sem.at[peer], out_recv_sem.at[here],
-            (me, peer),
-        )
-
-    def out_arrival(peer):
-        return remote(
-            out_send.at[peer], out_recv.at[peer], out_send_sem.at[peer], out_recv_sem.at[peer],
-            (me, peer),
+            out_send.at[peer], out_recv.at[here], send_sem.at[2], out_recv_sem.at[0], (me, peer)
         )
 
     def back_copy(j, peer):
         return remote(
             back_send.at[j, peer], back_recv.at[j, here],
-            back_send_sem.at[j, peer], back_recv_sem.at[j, here], (me, peer),
-        )
-
-    def back_arrival(j, peer):
-        return remote(
-            back_send.at[j, peer], back_recv.at[j, peer],
-            back_send_sem.at[j, peer], back_recv_sem.at[j, peer], (me, peer),
-        )
-
-    others = [lax.rem(here + k, stages) for k in range(1, stages)]
+            send_sem.at[3 + j], back_recv_sem.at[j], (me, peer),
+        )
+
     for j in range(stages - 1):
         out_copy(far_peer(j)).start()
     out_recv[here] = out_send[here]
@@ -472,42 +458,52 @@
     keep(signal_spec, unshifted(signal_waves))
     keep(hidden_spec, unshifted(spec))
 
-    loads["rows"].wait()
-    loads["ids"].wait()
-    blocks = rows_ref.shape[0]
-    draws = rows_ref.shape[1]
+    loaded(5, rows_ref)
+    loaded(6, ids_ref)
+    blocks, draws = rows_ref.shape
     block_size = segment // blocks
-    frame_block = lax.broadcasted_iota(jnp.int32, (draws, segment), 1) // block_size
-    counts = jnp.zeros((records * segment, segment), F32)
-    position = lax.broadcasted_iota(jnp.int32, (records * segment, draws), 0)
-    for b in range(blocks):
-        matches = jnp.where(position == rows_ref[b : b + 1, :], 1.0, 0.0).astype(BF16)
-        chosen = jnp.where(frame_block == b, 1.0, 0.0).astype(BF16)
-        counts += jnp.dot(matches, chosen, preferred_element_type=F32)
-    for c in range(chips):
-        counts_ref[c] = counts[c * 2 * segment : (c + 1) * 2 * segment, :]
-
-    loads["targets"].wait()
-    normalize(me)
-    self_units = units_ref[me].astype(F32).T
-    pass_arrival(6).wait_recv()
-    normalize(partner)
-    for n in (2, 3):
+    span = drawn_ref.shape[0] // blocks
+    place = lax.broadcasted_iota(jnp.int32, (span, draws), 0)
+    diagonal = place == lax.broadcasted_iota(jnp.int32, (span, draws), 1)
+    padding = lax.broadcasted_iota(jnp.int32, (span, 1), 0) >= draws
+    drawn = jnp.concatenate(
+        [
+            jnp.sum(
+                jnp.where(diagonal, rows_ref[b : b + 1, :].astype(F32), 0.0), axis=1, keepdims=True
+            )
+            - jnp.where(padding, 1.0, 0.0)
+            for b in range(blocks)
+        ],
+        axis=0,
+    )
+    own_id = ids_ref[me]
+    allowed = jnp.zeros_like(drawn)
+    for q in range(records):
+        inside = (drawn >= q * segment) & (drawn < (q + 1) * segment)
+        allowed += jnp.where(inside, jnp.where(ids_ref[q] != own_id, 1.0, 0.0).astype(F32), 0.0)
+    grid = (blocks * span, segment)
+    row_block = lax.broadcasted_iota(jnp.int32, grid, 0) // span
+    frame_block = lax.broadcasted_iota(jnp.int32, grid, 1) // block_size
+    mask = jnp.where(row_block == frame_block, allowed, 0.0)
+    lane = lax.broadcasted_iota(jnp.int32, (blocks * span, 2 * segment), 1).astype(F32)
+
+    def gathered(c):
+        units = pool[pl.ds(c * 2, 2)].reshape(2 * segment, depth)
+        first_row = (c * (2 * segment)).astype(F32)
+        chosen = jnp.where(drawn - first_row == lane, 1.0, 0.0).astype(BF16)
+        return jnp.dot(chosen, units, preferred_element_type=F32)
+
+    loaded(7, pool.at[me])
+    self_units = normalized(pool[me].astype(F32)).astype(F32).T
+    landed(pool.at[0], pass_recv_sem.at[0])
+    drawn_ref[...] = gathered(chip)
+    for n in (2, 3, 4, 5):
         pool_arrival(n).wait_recv()
         pass_copy(n).start()
-    for c in (x_chip, y_chip):
-        normalize(c * 2 + core)
-    for n in (1, 0, 2, 3):
-        pass_arrival(n).wait_recv()
-    for c in (x_chip, y_chip):
-        normalize(c * 2 + 1 - core)
-    for n in (4, 5):
-        pool_arrival(n).wait_recv()
-        pass_copy(n).start()
-    normalize(d_chip * 2 + core)
-
-    for peer in others:
-        out_arrival(peer).wait_recv()
+    landed(pool.at[pl.ds(0, 2)], pass_recv_sem.at[1])
+    drawn_ref[...] += gathered(x_chip) + gathered(y_chip)
+
+    landed(out_recv.at[pl.ds(0, stages - 1)], out_recv_sem.at[0])
     rows = jnp.concatenate([out_recv[s] for s in range(stages)], axis=0).astype(F32)
     radius = jnp.sqrt(jnp.sum(rows * rows, axis=0, keepdims=True) + EPSILON)
     unit_rows = rows * (1.0 / radius)
@@ -515,34 +511,14 @@
     positive = jnp.exp(jnp.sum(anchors.astype(F32) * self_units, axis=0, keepdims=True) * INVERSE_TEMP)
     alignment = jnp.sum(unit_rows * self_units, axis=0, keepdims=True)
 
-    upper = lax.broadcasted_iota(jnp.int32, (2 * segment, 1), 0) < segment
-
-    def against(c):
-        units = units_ref[pl.ds(c * 2, 2)].reshape(2 * segment, depth)
-        own_id = ids_ref[me]
-        allowed = [jnp.where(ids_ref[c * 2 + i] != own_id, 1.0, 0.0).astype(F32) for i in (0, 1)]
-        cosines = jnp.dot(units, anchors, preferred_element_type=F32)
-        weights = (
-            counts_ref[c] * jnp.where(upper, allowed[0], allowed[1]) * jnp.exp(cosines * INVERSE_TEMP)
-        )
-        rounded = weights.astype(BF16)
-        return (
-            jnp.sum(weights, axis=0, keepdims=True),
-            jnp.sum(rounded.astype(F32) * cosines, axis=0, keepdims=True),
-            jnp.dot(weights.T.astype(BF16), units, preferred_element_type=F32),
-        )
-
-    summed, turned, numerator = against(chip)
-    totals = positive + summed
-    for c in (x_chip, y_chip, d_chip):
-        if c is d_chip:
-            for n in (4, 5):
-                pass_arrival(n).wait_recv()
-            normalize(c * 2 + 1 - core)
-        summed, partial_turned, partial = against(c)
-        totals += summed
-        turned += partial_turned
-        numerator += partial
+    landed(pool.at[0], pass_recv_sem.at[2])
+    negatives = normalized(drawn_ref[...] + gathered(d_chip))
+    cosines = jnp.dot(negatives, anchors, preferred_element_type=F32)
+    weights = mask * jnp.exp(cosines * INVERSE_TEMP)
+    rounded = weights.astype(BF16)
+    totals = positive + jnp.sum(weights, axis=0, keepdims=True)
+    turned = jnp.sum(rounded.astype(F32) * cosines, axis=0, keepdims=True)
+    numerator = jnp.dot(weights.T.astype(BF16), negatives, preferred_element_type=F32)
     scale = INVERSE_TEMP * LOSS_SCALE / radius
     pull = (positive / totals - 1.0) * scale
     push = scale / totals
@@ -554,6 +530,8 @@
             back_send[j, s] = (
                 pull * self_units[at] + push * numerator[:, at].T - tilt * unit_rows[at]
             ).astype(BF16)
+        if j:
+            sent(back_send.at[j - 1, pl.ds(0, stages - 1)], send_sem.at[2 + j])
         for i in range(stages - 1):
             back_copy(j, far_peer(i)).start()
         back_recv[j, here] = back_send[j, here]
@@ -564,7 +542,7 @@
     def pair_copy(which, j, lane):
         return remote(
             pair_send.at[which, j, lane], pair_recv.at[which, j],
-            pair_send_sem.at[which, j], pair_recv_sem.at[which, j], (partner, here),
+            send_sem.at[3 + chunks], pair_recv_sem.at[which, j], (partner, here),
         )
 
     def spread(which, j, update):
@@ -575,12 +553,11 @@
     def ring_copy(which, j, n):
         return remote(
             ring_send.at[which, j, near[n]], ring_recv.at[which, j, n],
-            ring_send_sem.at[which, j, n], ring_recv_sem.at[which, j, n],
-            (near[n] * 2 + core, here),
+            send_sem.at[4 + chunks], ring_recv_sem.at[which, j], (near[n] * 2 + core, here),
         )
 
     def gather(which, j):
-        pair_copy(which, j, core).wait_recv()
+        landed(pair_recv.at[which, j], pair_recv_sem.at[which, j])
         joined = pair_send[which, j, core].astype(F32) + pair_recv[which, j].astype(F32)
         for c in range(chips):
             ring_send[which, j, c] = joined[c * shard : (c + 1) * shard, :].astype(BF16)
@@ -592,51 +569,33 @@
     def share_copy(which, j, n):
         block = targets_out[which].at[j, core, chip]
         return remote(
-            block, block, share_send_sem.at[which, j, n], share_recv_sem.at[which, j, n],
+            block, block, send_sem.at[5 + chunks], share_recv_sem.at[which, j],
             (near[n] * 2 + core, here),
         )
 
-    def share_arrival(which, j, n):
-        block = targets_out[which].at[j, core, near[n]]
-        return remote(
-            block, block, share_send_sem.at[which, j, n], share_recv_sem.at[which, j, n],
-            (near[n] * 2 + core, here),
-        )
-
-    sources = near + (chip,)
-
-    def last_copy(which, j, n):
-        block = targets_out[which].at[j, core, sources[n]]
-        return remote(
-            block, block, last_send_sem.at[which, j, n], last_recv_sem.at[which, j, n],
-            (partner, here),
-        )
-
-    def last_arrival(which, j, n):
-        block = targets_out[which].at[j, 1 - core, sources[n]]
-        return remote(
-            block, block, last_send_sem.at[which, j, n], last_recv_sem.at[which, j, n],
-            (partner, here),
+    def last_copy(which, j, owner):
+        block = targets_out[which].at[j, core, owner]
+        return remote(
+            block, block, send_sem.at[6 + chunks], last_recv_sem.at[0], (partner, here)
         )
 
     def share(which, j):
+        landed(ring_recv.at[which, j], ring_recv_sem.at[which, j])
         total = ring_send[which, j, chip].astype(F32)
         for n in range(3):
-            ring_copy(which, j, n).wait_recv()
             total += ring_recv[which, j, n].astype(F32)
         targets_out[which][j, core, chip] = total.astype(BF16)
         for n in (2, 0, 1):
             share_copy(which, j, n).start()
-        last_copy(which, j, 3).start()
+        last_copy(which, j, chip).start()
 
     def relay(which, j):
+        landed(ring_recv.at[which, j], share_recv_sem.at[which, j])
         for n in range(3):
-            share_arrival(which, j, n).wait_recv()
-            last_copy(which, j, n).start()
+            last_copy(which, j, near[n]).start()
 
     def backward(j):
-        for peer in others:
-            back_arrival(j, peer).wait_recv()
+        landed(back_recv.at[j, pl.ds(0, stages - 1)], back_recv_sem.at[j])
         lines = slice(j * size, (j + 1) * size)
         cotangent = jnp.concatenate([back_recv[j, s] for s in range(stages)], axis=1).astype(F32)
         late_drive = cotangent * second_ref[lines].astype(F32)
@@ -652,22 +611,8 @@
 
     for j in range(chunks):
         backward(j)
-        if j:
-
-            @pl.when(core == 1)
-            def _():
-                gather(1, j - 1)
-                gather(0, j - 1)
-
-        if j + 1 < chunks:
-
-            @pl.when(core == 0)
-            def _():
-                gather(1, j)
-                gather(0, j)
-
-    for which in (1, 0):
-        gather(which, chunks - 1)
+        for which in (1, 0):
+            gather(which, j)
     for j in range(chunks):
         for which in (1, 0):
             share(which, j)
@@ -675,23 +620,15 @@
         for which in (1, 0):
             relay(which, j)
 
-    for n in range(6):
-        pool_copy(n).wait_send()
-    for n in range(7):
-        pass_copy(n).wait_send()
-    for peer in others:
-        out_copy(peer).wait_send()
-        for j in range(chunks):
-            back_copy(j, peer).wait_send()
-    for j in range(chunks):
-        for which in (1, 0):
-            pair_copy(which, j, 1 - core).wait_send()
-            for n in range(3):
-                ring_copy(which, j, n).wait_send()
-                share_copy(which, j, n).wait_send()
-            for n in range(4):
-                last_copy(which, j, n).wait_send()
-                last_arrival(which, j, n).wait_recv()
+    sent(pool.at[pl.ds(0, 3)], send_sem.at[0])
+    sent(pool.at[pl.ds(0, 4)], send_sem.at[1])
+    sent(out_send.at[pl.ds(0, stages - 1)], send_sem.at[2])
+    sent(back_send.at[chunks - 1, pl.ds(0, stages - 1)], send_sem.at[2 + chunks])
+    sent(pair_recv, send_sem.at[3 + chunks])
+    sent(ring_recv, send_sem.at[4 + chunks])
+    sent(ring_recv, send_sem.at[5 + chunks])
+    sent(pair_recv, send_sem.at[6 + chunks])
+    landed(pair_recv, last_recv_sem.at[0])
 
 
 def finish(
@@ -740,9 +677,7 @@
     update = pltpu.VMEM(gradient, BF16)
     exchange = pltpu.VMEM((stages, channels, segment), BF16)
     plane = pltpu.VMEM((channels, frames), F32)
-    narrow = pltpu.VMEM((channels, frames), BF16)
     spec = pltpu.VMEM((2, channels, frames), F32)
-    skip = pltpu.VMEM((1, channels), F32)
     back = pltpu.VMEM((CHUNKS, stages, size, segment), BF16)
     semaphores = pltpu.SemaphoreType.DMA
     results = pl.pallas_call(
@@ -751,24 +686,20 @@
         in_specs=[hbm] * 12,
         out_specs=(vmem,) * 5,
         scratch_shapes=[
-            narrow, narrow, narrow, plane, plane, skip, skip,
-            pltpu.VMEM((blocks, draws), jnp.int32),
+            pltpu.VMEM((3, channels, frames), BF16), pltpu.VMEM((2, channels, frames), F32),
+            pltpu.VMEM((2, 1, channels), F32), pltpu.VMEM((blocks, draws), jnp.int32),
             pltpu.SMEM((records,), jnp.int32), pltpu.VMEM(waves.shape, BF16),
             pltpu.VMEM(turn.shape, F32),
-            pltpu.VMEM((records, segment, depth), BF16), pltpu.VMEM((records, segment, depth), BF16),
+            pltpu.VMEM((records, segment, depth), BF16),
             exchange, exchange, back, back,
             pltpu.VMEM((2, CHUNKS, 2, half, frames), BF16), pltpu.VMEM((2, CHUNKS, half, frames), BF16),
             pltpu.VMEM((2, CHUNKS, chips, shard, frames), BF16),
             pltpu.VMEM((2, CHUNKS, 3, shard, frames), BF16),
             plane, plane, spec, spec, spec, spec,
-            pltpu.VMEM((chips, 2 * segment, segment), F32),
-            semaphores((12,)), semaphores((6,)), semaphores((6,)), semaphores((7,)), semaphores((7,)),
-            semaphores((stages,)), semaphores((stages,)),
-            semaphores((CHUNKS, stages)), semaphores((CHUNKS, stages)),
-            semaphores((2, CHUNKS)), semaphores((2, CHUNKS)),
-            semaphores((2, CHUNKS, 3)), semaphores((2, CHUNKS, 3)),
-            semaphores((2, CHUNKS, 3)), semaphores((2, CHUNKS, 3)),
-            semaphores((2, CHUNKS, 4)), semaphores((2, CHUNKS, 4)),
+            pltpu.VMEM((blocks * -(-draws // 128) * 128, depth), F32),
+            semaphores((8,)), semaphores((7 + CHUNKS,)), semaphores((6,)), semaphores((3,)),
+            semaphores((1,)), semaphores((CHUNKS,)), semaphores((2, CHUNKS)),
+            semaphores((2, CHUNKS)), semaphores((2, CHUNKS)), semaphores((1,)),
         ],
         compiler_params=pltpu.CompilerParams(
             collective_id=0, has_side_effects=True, vmem_limit_bytes=VMEM_BYTES

time: 38 us -> 37.1 us (0.976)
  Pallas kernels: 37.2 us -> 36.3 us
    pallas_call x1, Pallas kernels: 35.9 us -> 35.1 us  [local(): pl.pallas_call(functools.partial(kernel, (records, stages)), out_shape=(s...]
where the time goes in v3:
time: 37.1 us; the launch traced here: 37 us
  Pallas kernels  36.3 us (98%)
  between operations  0.64 us (2%)
    pallas_call x1, Pallas kernels, local(): pl.pallas_call(functools.partial(kernel, (records, stages)), out_shape=(s...  35.1 us
    pallas_call x1, Pallas kernels, local(): pl.pallas_call(functools.partial(finish, frames), out_shape=(jax.ShapeDty...  1.27 us

profile of v3, /device:TPU:0, one launch (start us, length us, event | category | flops | bytes accessed | tf_op | source)
XLA Modules:
  0.0 37.0 jit_solution(16827382833786377505)
XLA Ops:
  0.6 35.1 %shard_map.155 = (bf16[1,256,512]{2,1,0:T(8,128)(2,1)S(1)}, bf16[1,256,512]{2,1,0:T(8,128)(2,1)S(1)}, bf16[1,256,512]{2,1,0:T(8,128)(2,1)S(1)}, bf16[2,2,4,16,51...) custom-call(bf16[1,256,512]{2,1,0:T(8,128)(2,1)} %values_hbm.1, bf16[1,256,512]{2,1,0:T(8,128)(2,1)} %first_hbm.1, ...), custom_call_target="tpu_custom_call" | custom-call | tf_op jit(solution)/shard_map/pallas_call | solution.py:683
  35.7 1.3 %shard_map.156 = (bf16[1,256,512]{2,1,0:T(8,128)(2,1)}, bf16[1,256,512]{2,1,0:T(8,128)(2,1)}, bf16[1,256,512]{2,1,0:T(8,128)(2,1)}, f32[2,2,4,16,512]{4,3,2,1,0:T(8,128)}, f32[2,2,4,16,512]{4,3,2,1,0:T(8,128)}) custom-call(bf16[1,256,512]{2,1,0:T(8,128)(2,1)S(1)} %get-tuple-element.15.values_in, bf16[1,256,512]{2,1,0:T(8,128)(2,1)S(1)} %get-tuple-element.16.first_in, ...), custom_call_target="tpu_custom_call" | custom-call | tf_op jit(solution)/shard_map/pallas_call | solution.py:716

commit v4 on v3

--- a/solution.py
+++ b/solution.py
@@ -18,6 +18,9 @@
 TABLE_BYTES = 16 * 1024 * 1024
 INNER_WIDTH = 128
 GRID_CHIPS = 4
+FINE_FILTERS = True
+FINE_VALUES = True
+FINE_HIDDEN = False
 CHUNKS = 2
 VMEM_BYTES = 40 * 1024 * 1024
 HIGHEST = lax.Precision.HIGHEST
@@ -238,22 +241,28 @@
 
 
 def tables(frames):
-    odd = 2 * np.arange(frames, dtype=np.int64) + 1
-    period = 8 * frames
-    circle = 2.0 * np.pi / period * np.arange(period)
-    product = odd[:, None] * odd[None, :] % period
-    waves = np.stack([wave.astype(BF16)[product] for wave in (np.cos(circle), np.sin(circle))])
+    middle = frames // 2
+    order = np.concatenate([np.arange(0, frames, 2), np.arange(1, frames, 2)])
+    odd = 2 * order.astype(np.int64) + 1
+    product = odd[None, :] * (2 * np.arange(middle, dtype=np.int64) + 1)[:, None]
+    angle = np.pi / (4.0 * frames) * (product % (8 * frames))
+    plus, minus = np.cos(angle) + np.sin(angle), np.cos(angle) - np.sin(angle)
+    even = np.arange(frames) < middle
+    ahead = np.stack([np.where(even, plus, minus), np.where(even, minus, plus)]).astype(np.float32)
     half = np.pi * odd / (4.0 * frames)
-    turn = np.stack([np.cos(half), np.sin(half)]) / frames
-    return waves, turn.astype(np.float32)
+    both = np.stack([np.cos(half) + np.sin(half), np.cos(half) - np.sin(half)]) / (4.0 * frames)
+    turn = np.where(even, both, both[::-1]).astype(np.float32)
+    high = ahead.astype(BF16)
+    low = (ahead - high.astype(np.float32)).astype(BF16)
+    return np.concatenate([high, low]), np.swapaxes(high, 1, 2), turn
 
 
 def kernel(
     sizes,
     values_hbm, first_hbm, second_hbm, early_hbm, late_hbm, early_skip_hbm, late_skip_hbm,
-    targets_hbm, rows_hbm, ids_hbm, waves_hbm, turn_hbm,
+    targets_hbm, rows_hbm, ids_hbm, waves_hbm, inverse_hbm, turn_hbm,
     values_out, first_out, second_out, early_out, late_out,
-    streams_ref, filters_ref, skips_ref, rows_ref, ids_ref, waves_ref, turn_ref,
+    streams_ref, filters_ref, skips_ref, rows_ref, ids_ref, waves_ref, inverse_ref, turn_ref,
     pool, out_send, out_recv, back_send, back_recv, pair_send, pair_recv, ring_send, ring_recv,
     mixed_one, mixed_two, early_spec, late_spec, signal_spec, hidden_spec, drawn_ref,
     load_sem, send_sem, pool_recv_sem, pass_recv_sem, out_recv_sem, back_recv_sem,
@@ -296,6 +305,7 @@
             (5, rows_hbm.at[0], rows_ref),
             (6, ids_hbm, ids_ref),
             (7, targets_hbm.at[0], pool.at[me]),
+            (8, inverse_hbm, inverse_ref),
         )
     ]
     for load in loads:
@@ -318,69 +328,93 @@
     def landed(ref, sem):
         remote(ref, ref, sem, sem, (partner, here)).wait_recv()
 
-    def piece(owner, h):
-        return pool.at[owner * 2 + core, pl.ds(h * part, part)]
+    def piece(owner, start, count):
+        return pool.at[owner * 2 + core, pl.ds(start, count)]
+
+    quarter = part // 2
+    whole = ((part, part), (0, part), (0, part), (part, part))
+    quarters = ((0, quarter), (part, quarter), (quarter, quarter), (part + quarter, quarter))
+    spans = whole + quarters
+    lanes = (x_chip, y_chip, x_chip, y_chip) * 2
+    origins = (chip,) * 4 + (y_chip, x_chip) * 2
+    arrivals = (x_chip, y_chip, x_chip, y_chip) + (d_chip,) * 4
 
     def pool_copy(n):
-        owner, h, to = (
-            (chip, 1, x_chip), (chip, 0, y_chip), (chip, 0, x_chip), (chip, 1, y_chip),
-            (y_chip, 0, x_chip), (x_chip, 1, y_chip),
-        )[n]
-        block = piece(owner, h)
-        source = targets_hbm.at[0, pl.ds(h * part, part)] if n < 4 else block
+        block = piece(origins[n], *spans[n])
+        source = targets_hbm.at[0, pl.ds(*spans[n])] if n < 4 else block
         return remote(
-            source, block, send_sem.at[0], pool_recv_sem.at[n], (to * 2 + core, here)
+            source, block, send_sem.at[0], pool_recv_sem.at[n], (lanes[n] * 2 + core, here)
         )
 
     def pool_arrival(n):
-        owner, h, to = (
-            (x_chip, 1, x_chip), (y_chip, 0, y_chip), (x_chip, 0, x_chip), (y_chip, 1, y_chip),
-            (d_chip, 0, x_chip), (d_chip, 1, y_chip),
-        )[n]
-        block = piece(owner, h)
+        block = piece(arrivals[n], *spans[n])
         return remote(
-            block, block, send_sem.at[0], pool_recv_sem.at[n], (to * 2 + core, here)
+            block, block, send_sem.at[0], pool_recv_sem.at[n], (lanes[n] * 2 + core, here)
         )
 
     def pass_copy(n):
-        if n == 6:
-            block = pool.at[me]
-            return remote(
-                targets_hbm.at[0], block, send_sem.at[1], pass_recv_sem.at[0], (partner, here)
-            )
-        else:
-            owner, h = (
-                (x_chip, 1), (y_chip, 0), (x_chip, 0), (y_chip, 1), (d_chip, 0), (d_chip, 1)
-            )[n]
-            block = piece(owner, h)
+        block = piece(arrivals[n], *spans[n])
         return remote(
             block, block, send_sem.at[1], pass_recv_sem.at[1 + n // 4], (partner, here)
         )
 
     for n in range(4):
         pool_copy(n).start()
-    pass_copy(6).start()
+    remote(
+        targets_hbm.at[0], pool.at[me], send_sem.at[1], pass_recv_sem.at[0], (partner, here)
+    ).start()
 
     def normalized(rows):
         norm = jnp.sqrt(jnp.sum(rows * rows, axis=-1, keepdims=True) + EPSILON)
         return (rows * (1.0 / norm)).astype(BF16)
 
-    def forward(signal):
+    middle = frames // 2
+    flip_row = lax.broadcasted_iota(jnp.int32, (middle, middle), 0)
+    flip_column = lax.broadcasted_iota(jnp.int32, (middle, middle), 1)
+    mirror = jnp.where(flip_row + flip_column == middle - 1, 1.0, 0.0).astype(BF16)
+
+    def halves(value):
+        high = value.astype(BF16)
+        return high, (value - high.astype(F32)).astype(BF16)
+
+    def turned_over_wide(signal):
+        tail = sum(
+            jnp.dot(part, mirror, preferred_element_type=F32)
+            for part in halves(signal[:, middle:])
+        )
+        return jnp.concatenate([signal[:, :middle], tail], axis=1)
+
+    def turned_over(signal):
         signal = signal.astype(BF16)
-        return tuple(jnp.dot(signal, waves_ref[i], preferred_element_type=F32) for i in (0, 1))
-
-    def inverse(cosine, sine):
-        return jnp.dot(
-            cosine.astype(BF16), waves_ref[0], preferred_element_type=F32
-        ) + jnp.dot(sine.astype(BF16), waves_ref[1], preferred_element_type=F32)
+        tail = jnp.dot(signal[:, middle:], mirror, preferred_element_type=F32).astype(BF16)
+        return jnp.concatenate([signal[:, :middle], tail], axis=1)
+
+    def forward(signal, fine=False):
+        head, tail = signal[:, :middle].astype(F32), signal[:, middle:].astype(F32)
+        spec = []
+        for i, fold in enumerate((head + tail, head - tail)):
+            high, low = halves(fold)
+            wave = jnp.dot(high, waves_ref[i], preferred_element_type=F32)
+            if fine:
+                wave += jnp.dot(high, waves_ref[2 + i], preferred_element_type=F32)
+                wave += jnp.dot(low, waves_ref[i], preferred_element_type=F32)
+            spec.append(wave)
+        return tuple(spec)
+
+    def inverse(*spec):
+        plus, minus = (
+            jnp.dot(wave.astype(BF16), inverse_ref[i], preferred_element_type=F32)
+            for i, wave in enumerate(spec)
+        )
+        return jnp.concatenate([plus + minus, plus - minus], axis=1)
 
     def unshifted(spec):
-        cosine, sine = spec
-        turn_cosine = turn_ref[0:1, :]
-        turn_sine = turn_ref[1:2, :]
+        first, second = spec
+        turn_first = turn_ref[0:1, :]
+        turn_second = turn_ref[1:2, :]
         return (
-            cosine * turn_cosine + sine * turn_sine,
-            sine * turn_cosine - cosine * turn_sine,
+            first * turn_first + second * turn_second,
+            first * turn_second - second * turn_first,
         )
 
     def keep(ref, spec):
@@ -388,15 +422,15 @@
         ref[1] = spec[1]
 
     def convolved(spec, ref):
-        cosine, sine = spec
-        return inverse(cosine * ref[0] - sine * ref[1], cosine * ref[1] + sine * ref[0])
+        first, second = spec
+        return inverse(first * ref[0] + second * ref[1], second * ref[0] - first * ref[1])
 
     def correlated(spec, refs, lines):
-        cosine, sine = spec
+        first, second = spec
         waves = []
         for ref in refs:
             real, imaginary = ref[0, lines], ref[1, lines]
-            waves.append((cosine * real + sine * imaginary, sine * real - cosine * imaginary))
+            waves.append((first * real - second * imaginary, second * real + first * imaginary))
         joined = inverse(*(jnp.concatenate(wave, axis=0) for wave in zip(*waves)))
         count = joined.shape[0] // len(refs)
         return [joined[i * count : (i + 1) * count] for i in range(len(refs))]
@@ -407,23 +441,27 @@
     loaded(0, filters_ref)
     loaded(1, waves_ref)
     loaded(2, turn_ref)
-    keep(early_spec, unshifted(forward(filters_ref[0])))
-    keep(late_spec, unshifted(forward(filters_ref[1])))
+    keep(early_spec, unshifted(forward(turned_over_wide(filters_ref[0]), FINE_FILTERS)))
+    keep(late_spec, unshifted(forward(turned_over_wide(filters_ref[1]), FINE_FILTERS)))
     loaded(3, streams_ref)
     loaded(4, skips_ref)
     values_ref, first_ref, second_ref = (streams_ref.at[i] for i in range(3))
+    for ref in (values_ref, first_ref, second_ref):
+        ref[...] = turned_over(ref[...])
+    loaded(8, inverse_ref)
     early_skip = column(skips_ref[0])
     late_skip = column(skips_ref[1])
-    spec = forward(values_ref[...])
+    spec = forward(values_ref[...], FINE_VALUES)
     mixed_one[...] = convolved(spec, early_spec) + early_skip * values_ref[...].astype(F32)
     signal_waves = spec
     hidden = first_ref[...].astype(F32) * mixed_one[...]
-    spec = forward(hidden)
+    spec = forward(hidden, FINE_HIDDEN)
     mixed_two[...] = convolved(spec, late_spec) + late_skip * hidden
 
     output = second_ref[...].astype(F32) * mixed_two[...]
-    for s in range(stages):
-        out_send[s] = output[:, s * segment : (s + 1) * segment].astype(BF16)
+    order = [s if 2 * s < stages else stages - 1 - s + stages // 2 for s in range(stages)]
+    for i, s in enumerate(order):
+        out_send[s] = output[:, i * segment : (i + 1) * segment].astype(BF16)
 
     low_side = 1 - (2 * here) // stages
 
@@ -450,9 +488,11 @@
 
     pool_arrival(1).wait_recv()
     pool_copy(4).start()
+    pool_copy(6).start()
     pass_copy(1).start()
     pool_arrival(0).wait_recv()
     pool_copy(5).start()
+    pool_copy(7).start()
     pass_copy(0).start()
 
     keep(signal_spec, unshifted(signal_waves))
@@ -482,8 +522,10 @@
         inside = (drawn >= q * segment) & (drawn < (q + 1) * segment)
         allowed += jnp.where(inside, jnp.where(ids_ref[q] != own_id, 1.0, 0.0).astype(F32), 0.0)
     grid = (blocks * span, segment)
+    reverse = (2 * here) // stages
     row_block = lax.broadcasted_iota(jnp.int32, grid, 0) // span
-    frame_block = lax.broadcasted_iota(jnp.int32, grid, 1) // block_size
+    frame = lax.broadcasted_iota(jnp.int32, grid, 1)
+    frame_block = (frame + reverse * (segment - 1 - 2 * frame)) // block_size
     mask = jnp.where(row_block == frame_block, allowed, 0.0)
     lane = lax.broadcasted_iota(jnp.int32, (blocks * span, 2 * segment), 1).astype(F32)
 
@@ -494,10 +536,17 @@
         return jnp.dot(chosen, units, preferred_element_type=F32)
 
     loaded(7, pool.at[me])
-    self_units = normalized(pool[me].astype(F32)).astype(F32).T
+    own_row = lax.broadcasted_iota(jnp.int32, (segment, segment), 0)
+    own_column = lax.broadcasted_iota(jnp.int32, (segment, segment), 1)
+    arranged = own_column == own_row + reverse * (segment - 1 - 2 * own_row)
+    self_units = jnp.dot(
+        jnp.where(arranged, 1.0, 0.0).astype(BF16),
+        normalized(pool[me].astype(F32)),
+        preferred_element_type=F32,
+    ).T
     landed(pool.at[0], pass_recv_sem.at[0])
     drawn_ref[...] = gathered(chip)
-    for n in (2, 3, 4, 5):
+    for n in range(2, 8):
         pool_arrival(n).wait_recv()
         pass_copy(n).start()
     landed(pool.at[pl.ds(0, 2)], pass_recv_sem.at[1])
@@ -512,13 +561,14 @@
     alignment = jnp.sum(unit_rows * self_units, axis=0, keepdims=True)
 
     landed(pool.at[0], pass_recv_sem.at[2])
-    negatives = normalized(drawn_ref[...] + gathered(d_chip))
-    cosines = jnp.dot(negatives, anchors, preferred_element_type=F32)
+    wide = drawn_ref[...] + gathered(d_chip)
+    negatives = wide.astype(BF16)
+    shrink = 1.0 / jnp.sqrt(jnp.sum(wide * wide, axis=-1, keepdims=True) + EPSILON)
+    cosines = shrink * jnp.dot(negatives, anchors, preferred_element_type=F32)
     weights = mask * jnp.exp(cosines * INVERSE_TEMP)
-    rounded = weights.astype(BF16)
     totals = positive + jnp.sum(weights, axis=0, keepdims=True)
-    turned = jnp.sum(rounded.astype(F32) * cosines, axis=0, keepdims=True)
-    numerator = jnp.dot(weights.T.astype(BF16), negatives, preferred_element_type=F32)
+    turned = jnp.sum(weights * cosines, axis=0, keepdims=True)
+    numerator = jnp.dot((weights * shrink).T.astype(BF16), negatives, preferred_element_type=F32)
     scale = INVERSE_TEMP * LOSS_SCALE / radius
     pull = (positive / totals - 1.0) * scale
     push = scale / totals
@@ -531,7 +581,11 @@
                 pull * self_units[at] + push * numerator[:, at].T - tilt * unit_rows[at]
             ).astype(BF16)
         if j:
-            sent(back_send.at[j - 1, pl.ds(0, stages - 1)], send_sem.at[2 + j])
+
+            @pl.when(core == 1)
+            def _():
+                sent(back_send.at[j - 1, pl.ds(0, stages - 1)], send_sem.at[2 + j])
+
         for i in range(stages - 1):
             back_copy(j, far_peer(i)).start()
         back_recv[j, here] = back_send[j, here]
@@ -546,8 +600,9 @@
         )
 
     def spread(which, j, update):
+        update = turned_over(update)
         for i in (0, 1):
-            pair_send[which, j, i] = update[i * half : (i + 1) * half, :].astype(BF16)
+            pair_send[which, j, i] = update[i * half : (i + 1) * half, :]
         pair_copy(which, j, 1 - core).start()
 
     def ring_copy(which, j, n):
@@ -597,7 +652,7 @@
     def backward(j):
         landed(back_recv.at[j, pl.ds(0, stages - 1)], back_recv_sem.at[j])
         lines = slice(j * size, (j + 1) * size)
-        cotangent = jnp.concatenate([back_recv[j, s] for s in range(stages)], axis=1).astype(F32)
+        cotangent = jnp.concatenate([back_recv[j, s] for s in order], axis=1).astype(F32)
         late_drive = cotangent * second_ref[lines].astype(F32)
         update, adjoint = correlated(forward(late_drive), (hidden_spec, late_spec), lines)
         spread(1, j, update)
@@ -605,14 +660,14 @@
         early_drive = hidden_grad * first_ref[lines].astype(F32)
         update, adjoint = correlated(forward(early_drive), (signal_spec, early_spec), lines)
         spread(0, j, update)
-        values_out[0, lines] = (adjoint + early_skip[lines] * early_drive).astype(BF16)
-        second_out[0, lines] = (cotangent * mixed_two[lines]).astype(BF16)
-        first_out[0, lines] = (hidden_grad * mixed_one[lines]).astype(BF16)
+        for which in (1, 0):
+            gather(which, j)
+        values_out[0, lines] = turned_over(adjoint + early_skip[lines] * early_drive)
+        second_out[0, lines] = turned_over(cotangent * mixed_two[lines])
+        first_out[0, lines] = turned_over(hidden_grad * mixed_one[lines])
 
     for j in range(chunks):
         backward(j)
-        for which in (1, 0):
-            gather(which, j)
     for j in range(chunks):
         for which in (1, 0):
             share(which, j)
@@ -623,6 +678,12 @@
     sent(pool.at[pl.ds(0, 3)], send_sem.at[0])
     sent(pool.at[pl.ds(0, 4)], send_sem.at[1])
     sent(out_send.at[pl.ds(0, stages - 1)], send_sem.at[2])
+    for j in range(1, chunks):
+
+        @pl.when(core == 0)
+        def _():
+            sent(back_send.at[j - 1, pl.ds(0, stages - 1)], send_sem.at[2 + j])
+
     sent(back_send.at[chunks - 1, pl.ds(0, stages - 1)], send_sem.at[2 + chunks])
     sent(pair_recv, send_sem.at[3 + chunks])
     sent(ring_recv, send_sem.at[4 + chunks])
@@ -659,12 +720,12 @@
 ):
     _, channels, frames = values.shape
     _, segment, depth = targets.shape
-    if 8 * frames * frames > TABLE_BYTES or records != 2 * GRID_CHIPS:
+    if 8 * frames * frames > TABLE_BYTES or records != 2 * GRID_CHIPS or stages % 2:
         return local_large(
             values, gates_first, gates_second, filter_early, filter_late, skip_early, skip_late,
             targets, negative_rows, recording_ids,
         )
-    waves, turn = tables(frames)
+    waves, inverse_waves, turn = tables(frames)
     chips = records // 2
     size = channels // CHUNKS
     half = size // 2
@@ -683,12 +744,13 @@
     results = pl.pallas_call(
         functools.partial(kernel, (records, stages)),
         out_shape=(stream, stream, stream, update, update),
-        in_specs=[hbm] * 12,
+        in_specs=[hbm] * 13,
         out_specs=(vmem,) * 5,
         scratch_shapes=[
             pltpu.VMEM((3, channels, frames), BF16), pltpu.VMEM((2, channels, frames), F32),
             pltpu.VMEM((2, 1, channels), F32), pltpu.VMEM((blocks, draws), jnp.int32),
             pltpu.SMEM((records,), jnp.int32), pltpu.VMEM(waves.shape, BF16),
+            pltpu.VMEM(inverse_waves.shape, BF16),
             pltpu.VMEM(turn.shape, F32),
             pltpu.VMEM((records, segment, depth), BF16),
             exchange, exchange, back, back,
@@ -697,7 +759,7 @@
             pltpu.VMEM((2, CHUNKS, 3, shard, frames), BF16),
             plane, plane, spec, spec, spec, spec,
             pltpu.VMEM((blocks * -(-draws // 128) * 128, depth), F32),
-            semaphores((8,)), semaphores((7 + CHUNKS,)), semaphores((6,)), semaphores((3,)),
+            semaphores((9,)), semaphores((7 + CHUNKS,)), semaphores((8,)), semaphores((3,)),
             semaphores((1,)), semaphores((CHUNKS,)), semaphores((2, CHUNKS)),
             semaphores((2, CHUNKS)), semaphores((2, CHUNKS)), semaphores((1,)),
         ],
@@ -709,7 +771,7 @@
         for operand in (
             values, gates_first, gates_second, filter_early, filter_late,
             skip_early[None], skip_late[None], targets, negative_rows, recording_ids,
-            jnp.asarray(waves), jnp.asarray(turn),
+            jnp.asarray(waves), jnp.asarray(inverse_waves), jnp.asarray(turn),
         )
     ))
     wide = gradient

time: 37.1 us -> 36.7 us (0.989)
  Pallas kernels: 36.3 us -> 35.9 us
    pallas_call x1, Pallas kernels: 35.1 us -> 34.7 us  [local(): pl.pallas_call(functools.partial(kernel, (records, stages)), out_shape=(s...]
where the time goes in v4:
time: 36.7 us; the launch traced here: 36.6 us
  Pallas kernels  35.9 us (98%)
  between operations  0.64 us (2%)
    pallas_call x1, Pallas kernels, local(): pl.pallas_call(functools.partial(kernel, (records, stages)), out_shape=(s...  34.7 us
    pallas_call x1, Pallas kernels, local(): pl.pallas_call(functools.partial(finish, frames), out_shape=(jax.ShapeDty...  1.27 us

profile of v4, /device:TPU:0, one launch (start us, length us, event | category | flops | bytes accessed | tf_op | source)
XLA Modules:
  0.0 36.6 jit_solution(13110902285687098430)
XLA Ops:
  0.6 34.7 %shard_map.164 = (bf16[1,256,512]{2,1,0:T(8,128)(2,1)S(1)}, bf16[1,256,512]{2,1,0:T(8,128)(2,1)S(1)}, bf16[1,256,512]{2,1,0:T(8,128)(2,1)S(1)}, bf16[2,2,4,16,51...) custom-call(bf16[1,256,512]{2,1,0:T(8,128)(2,1)} %values_hbm.1, bf16[1,256,512]{2,1,0:T(8,128)(2,1)} %first_hbm.1, ...), custom_call_target="tpu_custom_call" | custom-call | tf_op jit(solution)/shard_map/pallas_call | solution.py:744
  35.3 1.3 %shard_map.165 = (bf16[1,256,512]{2,1,0:T(8,128)(2,1)}, bf16[1,256,512]{2,1,0:T(8,128)(2,1)}, bf16[1,256,512]{2,1,0:T(8,128)(2,1)}, f32[2,2,4,16,512]{4,3,2,1,0:T(8,128)}, f32[2,2,4,16,512]{4,3,2,1,0:T(8,128)}) custom-call(bf16[1,256,512]{2,1,0:T(8,128)(2,1)S(1)} %get-tuple-element.15.values_in, bf16[1,256,512]{2,1,0:T(8,128)(2,1)S(1)} %get-tuple-element.16.first_in, ...), custom_call_target="tpu_custom_call" | custom-call | tf_op jit(solution)/shard_map/pallas_call | solution.py:778

commit v5 on v4

--- a/solution.py
+++ b/solution.py
@@ -360,9 +360,6 @@
 
     for n in range(4):
         pool_copy(n).start()
-    remote(
-        targets_hbm.at[0], pool.at[me], send_sem.at[1], pass_recv_sem.at[0], (partner, here)
-    ).start()
 
     def normalized(rows):
         norm = jnp.sqrt(jnp.sum(rows * rows, axis=-1, keepdims=True) + EPSILON)
@@ -486,6 +483,9 @@
         out_copy(far_peer(j)).start()
     out_recv[here] = out_send[here]
 
+    remote(
+        targets_hbm.at[0], pool.at[me], send_sem.at[1], pass_recv_sem.at[0], (partner, here)
+    ).start()
     pool_arrival(1).wait_recv()
     pool_copy(4).start()
     pool_copy(6).start()
@@ -658,17 +658,24 @@
         spread(1, j, update)
         hidden_grad = adjoint + late_skip[lines] * late_drive
         early_drive = hidden_grad * first_ref[lines].astype(F32)
-        update, adjoint = correlated(forward(early_drive), (signal_spec, early_spec), lines)
-        spread(0, j, update)
+        spec = forward(early_drive)
+        spread(0, j, correlated(spec, (signal_spec,), lines)[0])
         for which in (1, 0):
             gather(which, j)
-        values_out[0, lines] = turned_over(adjoint + early_skip[lines] * early_drive)
-        second_out[0, lines] = turned_over(cotangent * mixed_two[lines])
-        first_out[0, lines] = turned_over(hidden_grad * mixed_one[lines])
-
-    for j in range(chunks):
-        backward(j)
-    for j in range(chunks):
+        def outs():
+            adjoint = correlated(spec, (early_spec,), lines)[0]
+            values_out[0, lines] = turned_over(adjoint + early_skip[lines] * early_drive)
+            second_out[0, lines] = turned_over(cotangent * mixed_two[lines])
+            first_out[0, lines] = turned_over(hidden_grad * mixed_one[lines])
+
+        return outs
+
+    results = [backward(j) for j in range(chunks)]
+    for which in (1, 0):
+        share(which, 0)
+    for result in results:
+        result()
+    for j in range(1, chunks):
         for which in (1, 0):
             share(which, j)
     for j in range(chunks):

time: 36.7 us -> 36.7 us (level)
  no operation moved by 1% of the time
where the time goes in v5:
time: 36.7 us; the launch traced here: 36.6 us
  Pallas kernels  35.9 us (98%)
  between operations  0.64 us (2%)
    pallas_call x1, Pallas kernels, local(): pl.pallas_call(functools.partial(kernel, (records, stages)), out_shape=(s...  34.7 us
    pallas_call x1, Pallas kernels, local(): pl.pallas_call(functools.partial(finish, frames), out_shape=(jax.ShapeDty...  1.27 us

profile of v5, /device:TPU:0, one launch (start us, length us, event | category | flops | bytes accessed | tf_op | source)
XLA Modules:
  0.0 36.6 jit_solution(6742611827737626126)
XLA Ops:
  0.6 34.7 %shard_map.164 = (bf16[1,256,512]{2,1,0:T(8,128)(2,1)S(1)}, bf16[1,256,512]{2,1,0:T(8,128)(2,1)S(1)}, bf16[1,256,512]{2,1,0:T(8,128)(2,1)S(1)}, bf16[2,2,4,16,51...) custom-call(bf16[1,256,512]{2,1,0:T(8,128)(2,1)} %values_hbm.1, bf16[1,256,512]{2,1,0:T(8,128)(2,1)} %first_hbm.1, ...), custom_call_target="tpu_custom_call" | custom-call | tf_op jit(solution)/shard_map/pallas_call | solution.py:751
  35.3 1.3 %shard_map.165 = (bf16[1,256,512]{2,1,0:T(8,128)(2,1)}, bf16[1,256,512]{2,1,0:T(8,128)(2,1)}, bf16[1,256,512]{2,1,0:T(8,128)(2,1)}, f32[2,2,4,16,512]{4,3,2,1,0:T(8,128)}, f32[2,2,4,16,512]{4,3,2,1,0:T(8,128)}) custom-call(bf16[1,256,512]{2,1,0:T(8,128)(2,1)S(1)} %get-tuple-element.15.values_in, bf16[1,256,512]{2,1,0:T(8,128)(2,1)S(1)} %get-tuple-element.16.first_in, ...), custom_call_target="tpu_custom_call" | custom-call | tf_op jit(solution)/shard_map/pallas_call | solution.py:785
